TPU v7x, 256 devices: a whole 4x4x8 slice. The times are simulated.
256 devices in a mesh: ia: 4 (over y), ja: 4 (over x), ka: 16 (over z, core).
Axes of the slice: x: 4, y: 4, z: 8, core: 2. Of those that a mesh axis runs over, the one named last changes fastest.
Arguments:
- blocks: bfloat16 [4, 4, 16, 2, 128, 128, 128], P('ia', 'ja', 'ka'), may hold values from -6 to 6
- first_mode_rows: int32 [4, 4, 16, 2], P('ia', 'ja', 'ka'), may hold values from 0 to 15
- second_mode_rows: int32 [4, 4, 16, 2], P('ia', 'ja', 'ka'), may hold values from 0 to 15
- third_mode_rows: int32 [4, 4, 16, 2], P('ia', 'ja', 'ka'), may hold values from 0 to 3
- filled: int32 [4, 4, 16], P('ia', 'ja', 'ka'), may hold values from 1 to 2, as said below
- owner_one: int32 [64], replicated, may hold values from 0 to 63, each once
- owner_two: int32 [64], replicated, may hold values from 0 to 63, each once
- factor_b: float32 [4, 2048, 256], P('ja', ('ia', 'ka'))
- factor_c: float32 [16, 512, 256], P('ka')
Outputs:
- a_new: float32 [4, 2048, 256], P('ia', ('ja', 'ka'))
- b_new: float32 [4, 2048, 256], P('ja', ('ia', 'ka'))
Inputs may be any that keep to these rules, and one draw needn't show every extreme that they name: Number of nonempty slots of a grid cell; at least one cell has all 2 slots filled. Slots at or beyond this count hold data that is not part of the tensor.
All inputs are finite; a program needn't handle non-finite values.
Results may differ from a plain program's by a relative error of at most 0.0039.
The roundings to bfloat16 on the way count: a program that leaves them out, or rounds other values in their place, can miss the bound.
Values may be sent and summed in bfloat16 or wider, within the bound.
A program may use at most 128 MiB of HBM per device.

v0:
```python
import jax
import jax.numpy as jnp
from jax import lax
from jax.sharding import PartitionSpec as P

EPS = 1e-06


def solve_rows(gram, rows):
    lower = jnp.linalg.cholesky(gram)
    return jax.scipy.linalg.cho_solve((lower, True), rows.T).T


def add_rows(accum, start, contrib):
    current = lax.dynamic_slice_in_dim(accum, start, contrib.shape[0], 0)
    return lax.dynamic_update_slice_in_dim(accum, current + contrib, start, 0)


def batched_sum(inner, weights):
    summed = lax.dot_general(
        inner,
        weights.astype(jnp.float32),
        (((1,), (0,)), ((2,), (1,))),
        precision=lax.Precision.HIGHEST,
        preferred_element_type=jnp.float32,
    )
    return summed.T


def to_logical(stored, owner, piece_rows):
    return stored.reshape(-1, piece_rows, stored.shape[1])[owner].reshape(stored.shape)


def to_stored(logical, owner, piece_rows):
    positions = jnp.arange(owner.shape[0], dtype=jnp.int32)
    inverse = jnp.sum(
        jnp.where(owner[None, :] == positions[:, None], positions[None, :], 0), axis=1
    )
    return logical.reshape(-1, piece_rows, logical.shape[1])[inverse].reshape(logical.shape)


def keep_same(value):
    return value


def partial_value(function, slot):

    def applied(value):
        return function(value, slot)

    return applied


def body(
    blocks,
    first_mode_rows,
    second_mode_rows,
    third_mode_rows,
    filled,
    owner_one,
    owner_two,
    factor_b,
    factor_c,
):
    highest = lax.Precision.HIGHEST
    piece_rows = factor_b.shape[1]
    rank_width = factor_b.shape[2]
    block_edge = blocks.shape[-1]
    slot_count = blocks.shape[3]
    total_one = piece_rows * lax.axis_size("ia") * lax.axis_size("ja") * lax.axis_size("ka")
    slab_rows_one = piece_rows * lax.axis_size("ja") * lax.axis_size("ka")
    slab_rows_two = piece_rows * lax.axis_size("ia") * lax.axis_size("ka")
    own_b = factor_b[0]
    own_c = lax.dynamic_slice_in_dim(
        factor_c[0], lax.axis_index(("ia", "ja")) * piece_rows, piece_rows, 0
    )
    local_b = jnp.dot(own_b.T, own_b, precision=highest, preferred_element_type=jnp.float32)
    local_c = jnp.dot(own_c.T, own_c, precision=highest, preferred_element_type=jnp.float32)
    gram_b, gram_c = lax.psum((local_b, local_c), ("ia", "ja", "ka"))
    stored_b = lax.all_gather(factor_b.astype(jnp.bfloat16), ("ia", "ka"), axis=1, tiled=True)[0]
    half_b = to_logical(stored_b, owner_two, piece_rows)
    half_c = factor_c[0].astype(jnp.bfloat16)
    live_count = filled[0, 0, 0]

    def update_one(partial_sum, slot):
        block = blocks[0, 0, 0, slot]
        b_rows = lax.dynamic_slice_in_dim(
            half_b, second_mode_rows[0, 0, 0, slot] * block_edge, block_edge, 0
        )
        c_rows = lax.dynamic_slice_in_dim(
            half_c, third_mode_rows[0, 0, 0, slot] * block_edge, block_edge, 0
        )
        inner = jnp.dot(
            block.reshape(block_edge * block_edge, block_edge),
            c_rows,
            preferred_element_type=jnp.float32,
        )
        inner = inner.reshape(block_edge, block_edge, rank_width)
        contrib = batched_sum(inner, b_rows)
        return add_rows(partial_sum, first_mode_rows[0, 0, 0, slot] * block_edge, contrib)

    partial_one = jnp.zeros((slab_rows_one, rank_width), jnp.float32)
    for slot in range(slot_count):
        partial_one = lax.cond(
            slot < live_count, partial_value(update_one, slot), keep_same, partial_one
        )
    stored_one = to_stored(partial_one, owner_one, piece_rows)
    system_one = gram_b * gram_c
    summed_own = lax.psum_scatter(stored_one, ("ja", "ka"), scatter_dimension=0, tiled=True)
    a_hat = solve_rows(system_one, summed_own)
    squares_a = lax.psum(jnp.sum(a_hat * a_hat, axis=0), ("ia", "ja", "ka"))
    scale_a = jnp.sqrt(squares_a / total_one + EPS)
    a_own = a_hat / scale_a
    local_a = jnp.dot(a_own.T, a_own, precision=highest, preferred_element_type=jnp.float32)
    gram_a = lax.psum(local_a, ("ia", "ja", "ka"))
    stored_a = lax.all_gather(a_own.astype(jnp.bfloat16)[None], ("ja", "ka"), axis=1, tiled=True)[0]
    half_a = to_logical(stored_a, owner_one, piece_rows)

    def update_two(partial_sum, slot):
        block = blocks[0, 0, 0, slot]
        a_rows = lax.dynamic_slice_in_dim(
            half_a, first_mode_rows[0, 0, 0, slot] * block_edge, block_edge, 0
        )
        c_rows = lax.dynamic_slice_in_dim(
            half_c, third_mode_rows[0, 0, 0, slot] * block_edge, block_edge, 0
        )
        inner = lax.dot_general(
            block.reshape(block_edge, block_edge * block_edge),
            a_rows,
            (((0,), (0,)), ((), ())),
            preferred_element_type=jnp.float32,
        )
        inner = inner.reshape(block_edge, block_edge, rank_width)
        contrib = batched_sum(inner, c_rows)
        return add_rows(partial_sum, second_mode_rows[0, 0, 0, slot] * block_edge, contrib)

    partial_two = jnp.zeros((slab_rows_two, rank_width), jnp.float32)
    for slot in range(slot_count):
        partial_two = lax.cond(
            slot < live_count, partial_value(update_two, slot), keep_same, partial_two
        )
    stored_two = to_stored(partial_two, owner_two, piece_rows)
    summed_two = lax.psum_scatter(stored_two, ("ia", "ka"), scatter_dimension=0, tiled=True)
    b_hat = solve_rows(gram_a * gram_c, summed_two)
    squares_b = lax.psum(jnp.sum(b_hat * b_hat, axis=0), ("ia", "ja", "ka"))
    b_own = b_hat / jnp.sqrt(squares_b / total_one + EPS)
    return (a_own[None], b_own[None])


def solution(mesh):
    return jax.shard_map(
        body,
        mesh=mesh,
        in_specs=(
            P("ia", "ja", "ka", None, None, None, None),
            P("ia", "ja", "ka", None),
            P("ia", "ja", "ka", None),
            P("ia", "ja", "ka", None),
            P("ia", "ja", "ka"),
            P(),
            P(),
            P("ja", ("ia", "ka"), None),
            P("ka", None, None),
        ),
        out_specs=(P("ia", ("ja", "ka"), None), P("ja", ("ia", "ka"), None)),
        check_vma=False,
    )
```

profile of v0, /device:TPU:1, one launch (start us, length us, event | category | flops | bytes accessed | tf_op | source)
XLA Modules:
  0.0 827.5 jit_solution(4852424667202017735)
XLA Ops:
  9.5 2.0 fusion.34
  11.5 2.0 fusion.36
  17.5 75.5 %all-gather.4.cloned.1.call-done = bf16[1,2048,256]{2,1,0:T(8,128)(2,1)} async-done(((bf16[1,32,256]{2,1,0:T(8,128)(2,1)}), bf16[1,2048,256]{2,1,0:T(8,128)(2,1)}) %all-gather.4.cloned.1.call-update) | async-done | bytes 1048592 | tf_op jit(solution)/shard_map/all_gather | solution.py:80
  93.0 1.8 gather_fusion
  94.8 23.3 %conditional.4 = (f32[2048,256]{1,0:T(8,128)}) conditional(s32[]{:T(128)} %bitcast.41, () %tuple.54, (s32[1,1,1,2]{3,2,1,0:T(1,128)}, bf16[512,256]{1,0:T(8,128)(2,1)S(1)}, bf16[1,1,1,2,128,128,128]{6,5,4,3,2,1,0:T(8,128)(2,1)}, s32[1,1,1,2]{3,2,1,0:T(1,128)}, bf16[2048,256]{1,0:T(8,128)(2,1)S(1)}, /*index=5*/s32[1,1,1,2]{3,2,1,0:T(1,128)}) %tuple.134), branch_computations={%region_6.0_spmd, %region_7.0_spmd} | conditional | flops 1082130432 | bytes 83099928 | solution.py:104
  95.5 2.8 slice.76
  98.3 2.4 convolution_bitcast_fusion
  100.7 6.7 copy.52
  107.6 8.2 multiply_reduce_fusion
  118.1 3.6 gather_fusion.1
  122.1 149.6 %all-reduce.7.cloned.1.call-done = (f32[256,256]{0,1:T(8,128)}, f32[256,256]{0,1:T(8,128)}) async-done(((f32[256,256]{0,1:T(8,128)}, f32[256,256]{0,1:T(8,128)}), (f32[256,256]{0,1:T(8,128)}, f32[256,256]{0,1:T(8,128)})) %all-reduce.7.cloned.1.call-update) | async-done | bytes 524304 | tf_op jit(solution)/shard_map/psum | solution.py:79
  273.0 11.7 %cholesky.130 = f32[128,128]{1,0:T(8,128)S(1)} custom-call(f32[128,128]{1,0:T(8,128)S(1)} %cholesky.194), custom_call_target="Cholesky" | custom-call | tf_op jit(solution)/shard_map/jit(cholesky)/cholesky | solution.py:10
  284.7 9.8 %custom-call.15 = f32[1,128,128]{1,2,0:T(8,128)S(1)} custom-call(f32[1,128,128]{2,1,0:T(8,128)S(1)} %get-tuple-element.155), custom_call_target="InvertDiagBlocksLowerTriangular" | custom-call | tf_op jit(solution)/shard_map/jit(cholesky)/cholesky | solution.py:10
  295.0 11.7 %cholesky.147 = f32[128,128]{1,0:T(8,128)S(1)} custom-call(f32[128,128]{1,0:T(8,128)S(1)} %convolution_subtract_fusion.1), custom_call_target="Cholesky" | custom-call | tf_op jit(solution)/shard_map/jit(cholesky)/cholesky | solution.py:10
  308.8 14.6 %while.4 = (s32[]{:T(128)}, f32[256,256]{1,0:T(8,128)S(1)}, s32[2,2]{1,0:T(2,128)S(1)}, f32[2,128,128]{2,1,0:T(8,128)S(1)}, s32[]{:T(128)}) while((s32[]{:T(128)}, f32[256,256]{1,0:T(8,128)S(1)}, s32[2,2]{1,0:T(2,128)S(1)}, f32[2,128,128]{2,1,0:T(8,128)S(1)}, s32[]{:T(128)}) %tuple.103), condition=%wide.while_cond, body=%wide.while_body.sunk | while | flops 2 | bytes 131181 | solution.py:11
  323.4 19.7 %custom-call.16 = f32[2,128,128]{1,2,0:T(8,128)S(1)} custom-call(f32[2,128,128]{2,1,0:T(8,128)S(1)} %get-tuple-element.124), custom_call_target="InvertDiagBlocksLowerTriangular" | custom-call | tf_op jit(solution)/shard_map/jit(_cho_solve)/triangular_solve | solution.py:11
  345.9 78.0 %psum.37 = f32[256]{0:T(256)S(1)} all-reduce(f32[256]{0:T(256)S(1)} %multiply_reduce_fusion.5), channel_id=1, replica_groups=mesh['ia'=4,'ja'=4,'ka'=16] {'ia','ja','ka'}, use_global_device_ids=true, to_apply=%region_13.16 | all-reduce | flops 256 | bytes 2048 | tf_op jit(solution)/shard_map/psum | solution.py:111
  425.9 71.4 %all-gather.6.cloned.1.call-done = bf16[2048,256]{1,0:T(8,128)(2,1)} async-done(((bf16[32,256]{1,0:T(8,128)(2,1)}), bf16[2048,256]{1,0:T(8,128)(2,1)}) %all-gather.6.cloned.1.call-update) | async-done | bytes 1048592 | tf_op jit(solution)/shard_map/all_gather | solution.py:116
  497.3 1.8 gather_fusion.2
  499.2 23.6 %conditional.6 = (f32[2048,256]{1,0:T(8,128)}) conditional(s32[]{:T(128)} %bitcast.41, () %tuple.57, (s32[1,1,1,2]{3,2,1,0:T(1,128)S(1)}, bf16[2048,256]{1,0:T(8,128)(2,1)S(1)}, bf16[1,1,1,2,128,128,128]{6,5,4,3,2,1,0:T(8,128)(2,1)}, s32[1,1,1,2]{3,2,1,0:T(1,128)S(1)}, bf16[512,256]{1,0:T(8,128)(2,1)S(1)}, ...), branch_computations={%region_15.18_spmd, %region_16.19_spmd} | conditional | flops 1082130432 | bytes 83099800 | solution.py:139
  499.2 2.5 slice.84
  501.7 3.6 convolution_bitcast_fusion.2
  505.3 6.7 copy.55
  512.2 8.3 multiply_reduce_fusion.2
  523.0 3.7 gather_fusion.3
  526.7 150.5 %all-reduce.5.cloned.1.call-done = f32[256,256]{0,1:T(8,128)} async-done(((f32[256,256]{0,1:T(8,128)}), f32[256,256]{0,1:T(8,128)}) %all-reduce.5.cloned.1.call-update) | async-done | bytes 262160 | tf_op jit(solution)/shard_map/psum | solution.py:115
  678.3 11.7 %cholesky.164 = f32[128,128]{1,0:T(8,128)S(1)} custom-call(f32[128,128]{1,0:T(8,128)S(1)} %cholesky.197), custom_call_target="Cholesky" | custom-call | tf_op jit(solution)/shard_map/jit(cholesky)/cholesky | solution.py:10
  690.1 9.8 %custom-call.17 = f32[1,128,128]{1,2,0:T(8,128)S(1)} custom-call(f32[1,128,128]{2,1,0:T(8,128)S(1)} %get-tuple-element.151), custom_call_target="InvertDiagBlocksLowerTriangular" | custom-call | tf_op jit(solution)/shard_map/jit(cholesky)/cholesky | solution.py:10
  700.4 11.7 %cholesky.181 = f32[128,128]{1,0:T(8,128)S(1)} custom-call(f32[128,128]{1,0:T(8,128)S(1)} %convolution_subtract_fusion), custom_call_target="Cholesky" | custom-call | tf_op jit(solution)/shard_map/jit(cholesky)/cholesky | solution.py:10
  714.7 4.2 while.5
  718.9 19.7 %custom-call.18 = f32[2,128,128]{1,2,0:T(8,128)S(1)} custom-call(f32[2,128,128]{2,1,0:T(8,128)S(1)} %get-tuple-element.125), custom_call_target="InvertDiagBlocksLowerTriangular" | custom-call | tf_op jit(solution)/shard_map/jit(_cho_solve)/triangular_solve | solution.py:11
  741.5 77.8 %psum.39 = f32[256]{0:T(256)S(1)} all-reduce(f32[256]{0:T(256)S(1)} %multiply_reduce_fusion.4), channel_id=1, replica_groups=mesh['ia'=4,'ja'=4,'ka'=16] {'ia','ja','ka'}, use_global_device_ids=true, to_apply=%region_22.25 | all-reduce | flops 256 | bytes 2048 | tf_op jit(solution)/shard_map/psum | solution.py:145
  (109 shorter events, 31.6 us)
Async XLA Ops:
  8.0 85.0 %all-gather.4.cloned.1.call-start = ((), (), s32[]{:S(2)}) async-start(), calls=%async_computation.2 | async-start | bytes 1064960 | tf_op jit(solution)/shard_map/all_gather | solution.py:80
  9.4 262.2 %all-reduce.7.cloned.1.call-start = ((), (), s32[]{:S(2)}) async-start(), calls=%async_computation.7 | async-start | bytes 1048576 | tf_op jit(solution)/shard_map/psum | solution.py:79
  13.5 329.6 %reduce-scatter.3.cloned.1.call-start = ((), (), s32[]{:S(2)}) async-start(), calls=%async_computation.3 | async-start | bytes 2129920 | tf_op jit(solution)/shard_map/reduce_scatter | solution.py:109
  100.7 6.7 copy-start.4
  107.5 8.4 %copy-start.7 = (s32[1,1,1,2]{3,2,1,0:T(1,128)S(1)}, s32[1,1,1,2]{3,2,1,0:T(1,128)}, u32[]{:S(2)}) copy-start(s32[1,1,1,2]{3,2,1,0:T(1,128)} %get-tuple-element.85) | copy-start | bytes 28 | tf_op jit(solution)/shard_map/cond
  121.7 302.9 %copy-start.1 = (s32[64]{0:T(128)S(1)}, s32[64]{0:T(128)}, u32[]{:S(2)}) copy-start(s32[64]{0:T(128)} %param.25) | copy-start | bytes 772
  121.7 375.6 %all-gather.6.cloned.1.call-start = ((), (), s32[]{:S(2)}) async-start(), calls=%async_computation.6 | async-start | bytes 1064960 | tf_op jit(solution)/shard_map/all_gather | solution.py:116
  271.6 227.5 %copy-start.2 = (s32[1,1,1,2]{3,2,1,0:T(1,128)S(1)}, s32[1,1,1,2]{3,2,1,0:T(1,128)}, u32[]{:S(2)}) copy-start(s32[1,1,1,2]{3,2,1,0:T(1,128)} %param.23) | copy-start | bytes 28
  271.6 227.5 %copy-start.3 = (s32[1,1,1,2]{3,2,1,0:T(1,128)S(1)}, s32[1,1,1,2]{3,2,1,0:T(1,128)}, u32[]{:S(2)}) copy-start(s32[1,1,1,2]{3,2,1,0:T(1,128)} %param.22) | copy-start | bytes 28
  271.6 227.5 %copy-start.6 = (s32[1,1,1,2]{3,2,1,0:T(1,128)S(1)}, s32[1,1,1,2]{3,2,1,0:T(1,128)}, u32[]{:S(2)}) copy-start(s32[1,1,1,2]{3,2,1,0:T(1,128)} %param.21) | copy-start | bytes 28
  424.6 252.5 %all-reduce.5.cloned.1.call-start = ((), (), s32[]{:S(2)}) async-start(), calls=%async_computation.4 | async-start | bytes 524288 | tf_op jit(solution)/shard_map/psum | solution.py:115
  425.8 312.8 %reduce-scatter.5.cloned.1.call-start = ((), (), s32[]{:S(2)}) async-start(), calls=%async_computation.5 | async-start | bytes 2129920 | tf_op jit(solution)/shard_map/reduce_scatter | solution.py:143
  523.0 154.2 %copy-start = (f32[256,256]{0,1:T(8,128)S(1)}, f32[256,256]{0,1:T(8,128)}, u32[]{:S(2)}) copy-start(f32[256,256]{0,1:T(8,128)} %get-tuple-element.143) | copy-start | bytes 786436
Sparse Core Ops, SparseCore 0:
  12.2 80.7 all-gather.3
  121.9 159.2 reduce-scatter.2
  424.7 72.5 all-gather.5
  526.8 159.5 reduce-scatter.4
Sparse Core Ops, SparseCore 1:
  15.6 256.0 all-reduce.6
  431.4 245.7 all-reduce.4
where the time goes:
time: 837 us; the launch traced here: 827 us
  waiting for transfers between devices  447 us (53%)
  blocking collectives  156 us (19%)
  other arithmetic  133 us (16%)
  local copies, waits for them, and re-layouts  42.5 us (5%)
  between operations  19.3 us (2%)
  matrix products  17.4 us (2%)
  loops' own time  12.2 us (1%)
    psum x1, waiting for transfers between devices, body(): gram_a = lax.psum(local_a, ('ia', 'ja', 'ka'))  150 us
    psum x1, waiting for transfers between devices, body(): gram_b, gram_c = lax.psum((local_b, local_c), ('ia', 'ja', 'ka'))  150 us
    psum x1, blocking collectives, body(): squares_a = lax.psum(jnp.sum(a_hat * a_hat, axis=0), ('ia', 'ja', 'ka'))  78 us
    psum x1, blocking collectives, body(): squares_b = lax.psum(jnp.sum(b_hat * b_hat, axis=0), ('ia', 'ja', 'ka'))  77.8 us
    all_gather x1, waiting for transfers between devices, body(): lax.all_gather(factor_b.astype(jnp.bfloat16), ('ia', 'ka'), axis=1, tiled...  75.5 us
    all_gather x1, waiting for transfers between devices, body(): lax.all_gather(a_own.astype(jnp.bfloat16)[None], ('ja', 'ka'), axis=1, ti...  71.4 us
    another operation x13, other arithmetic, solve_rows(): lower = jnp.linalg.cholesky(gram)  68.6 us
    another operation x5, other arithmetic, solve_rows(): return jax.scipy.linalg.cho_solve((lower, True), rows.T).T  39.4 us
  transfers between devices with their start and end apart: 6, of which 4 were waited for; matrix products, arithmetic and copies ran while one was open for 22% of the time, Pallas kernels for 0%

commit v1 on v0

v1 whole, which is shorter than its diff:
```python
import functools

import jax
import jax.numpy as jnp
from jax import lax
from jax.experimental import pallas as pl
from jax.experimental.pallas import tpu as pltpu
from jax.sharding import PartitionSpec as P

EPS = 1e-06
HALF = 128
GROUP = 8
MESH = pl.DeviceIdType.MESH
F32 = jnp.float32


def rem(a, b):
    return lax.rem(a, jnp.int32(b))


def div(a, b):
    return lax.div(a, jnp.int32(b))


def dot(a, b):
    return jnp.dot(a, b, precision=lax.Precision.HIGHEST, preferred_element_type=F32)


def dot_nt(a, b):
    return lax.dot_general(
        a, b, (((1,), (1,)), ((), ())), precision=lax.Precision.HIGHEST, preferred_element_type=F32
    )


def inverse_half(mat):
    lane = lax.broadcasted_iota(jnp.int32, (GROUP, HALF), 1)
    sub = lax.broadcasted_iota(jnp.int32, (GROUP, HALF), 0)
    lane_rest = lax.broadcasted_iota(jnp.int32, (HALF - GROUP, HALF), 1)

    def step(_, mat):
        top, rest = mat[:GROUP], mat[GROUP:]
        for s in range(GROUP):
            column = jnp.broadcast_to(top[:, s : s + 1], (GROUP, HALF))
            inv = 1.0 / column[s : s + 1]
            row = jnp.where(lane[:1] == s, 1.0, top[s : s + 1]) * inv
            cleared = jnp.where(lane == s, 0.0, top)
            top = jnp.where(sub == s, row, cleared - column * row)
        out = jnp.where(lane_rest < GROUP, 0.0, rest)
        for s in range(GROUP):
            out = out - rest[:, s : s + 1] * top[s : s + 1]
        return pltpu.roll(jnp.concatenate([out, top], axis=0), HALF - GROUP, 1)

    return lax.fori_loop(0, HALF // GROUP, step, mat)


def kernel(
    sizes,
    third,
    rows_b,
    rows_a,
    spots_one,
    spots_two,
    x_hbm,
    b_own,
    c_slab,
    a_out,
    b_out,
    x_buf,
    inner,
    gathered_b,
    gathered_a,
    rows_f32,
    contrib,
    part1,
    core1,
    line1,
    zed1,
    part2,
    core2,
    line2,
    zed2,
    local1,
    gram1,
    mix1,
    full1,
    local2,
    gram2,
    mix2,
    full2,
    own1,
    own2,
    gram_c_own,
    sq_ka,
    sq_kb,
    sq_la,
    sq_lb,
    factor,
    copy_sem,
    send_sem,
    recv_sem,
):
    n_i, n_j, n_k = sizes
    n_z = n_k // 2
    piece, rank = b_own.shape
    edge = x_hbm.shape[-1]
    per_block = edge // piece
    total_rows = n_i * n_j * n_k * piece
    chunk = rank // n_k
    i, j, k = lax.axis_index("ia"), lax.axis_index("ja"), lax.axis_index("ka")
    core = rem(k, 2)
    z = div(k, 2)
    plane = i * n_j + j
    n_plane = n_i * n_j
    sends = []

    def send(src, dst, where, stage):
        pltpu.make_async_remote_copy(
            src_ref=src,
            dst_ref=dst,
            send_sem=send_sem.at[stage],
            recv_sem=recv_sem.at[stage],
            device_id=where,
            device_id_type=MESH,
        ).start()

    def arrived(like, stage):
        pltpu.make_async_copy(like, like, recv_sem.at[stage]).wait()

    def at_plane(g):
        return {"ia": div(g, n_j), "ja": rem(g, n_j)}

    def gather_z(buf, line, n_line, stage):
        mine = buf.at[(core * n_line + line) * n_z + z]

        def one(d, carry):
            send(mine, mine, {"ka": rem(z + d, n_z) * 2 + core}, stage)
            return carry

        lax.fori_loop(1, n_z, one, 0)
        sends.append((buf.at[pl.ds(0, n_z - 1)], stage))

    def gather_line(buf, axis, line, n_line, stage):
        arrived(buf.at[pl.ds(0, n_z - 1)], stage - 1)
        mine = buf.at[pl.ds((core * n_line + line) * n_z, n_z)]

        def one(d, carry):
            send(mine, mine, {axis: rem(line + d, n_line)}, stage)
            return carry

        lax.fori_loop(1, n_line, one, 0)
        sends.append((buf.at[pl.ds(0, (n_line - 1) * n_z)], stage))

    def gather_core(buf, n_line, stage):
        half = n_line * n_z
        arrived(buf.at[pl.ds(0, half - n_z)], stage - 1)
        mine = buf.at[pl.ds(core * half, half)]
        send(mine, mine, {"ka": z * 2 + 1 - core}, stage)
        sends.append((buf.at[pl.ds(0, half)], stage))

    def scatter_core(part, got, stage):
        half = got.shape[0]
        send(part.at[pl.ds((1 - core) * half, half)], got, {"ka": z * 2 + 1 - core}, stage)
        sends.append((got, stage))

    def scatter_line(part, got_core, got, axis, line, n_line, stage):
        arrived(got_core, stage - 1)
        half = n_line * n_z

        def add(p, carry):
            part[core * half + p] = part[core * half + p] + got_core[p]
            return carry

        lax.fori_loop(0, half, add, 0)

        def one(d, carry):
            to = rem(line + d, n_line)
            send(part.at[pl.ds(core * half + to * n_z, n_z)], got.at[d - 1], {axis: to}, stage)
            return carry

        lax.fori_loop(1, n_line, one, 0)
        sends.append((got, stage))

    def scatter_z(part, got_line, got, line, n_line, stage):
        arrived(got_line, stage - 1)
        base = (core * n_line + line) * n_z

        def add(p, carry):
            value = part[base + p]
            for d in range(n_line - 1):
                value = value + got_line[d, p]
            part[base + p] = value
            return carry

        lax.fori_loop(0, n_z, add, 0)

        def one(d, carry):
            to = rem(z + d, n_z)
            send(part.at[base + to], got.at[d - 1], {"ka": to * 2 + core}, stage)
            return carry

        lax.fori_loop(1, n_z, one, 0)
        sends.append((got, stage))

    def scatter_end(part, got, line, n_line, stage):
        arrived(got, stage - 1)
        value = part[(core * n_line + line) * n_z + z]
        for d in range(n_z - 1):
            value = value + got[d]
        return value

    def share_k(source, got, stage):
        def one(d, carry):
            send(source(rem(k + d, n_k)), got.at[d - 1], {"ka": rem(k + d, n_k)}, stage)
            return carry

        lax.fori_loop(1, n_k, one, 0)
        sends.append((got, stage))

    def share_plane(source, got, stage):
        def one(d, carry):
            send(source, got.at[d - 1], at_plane(rem(plane + d, n_plane)), stage)
            return carry

        lax.fori_loop(1, n_plane, one, 0)
        sends.append((got, stage))

    def total(value, got, stage):
        arrived(got, stage)
        return lax.fori_loop(0, got.shape[0], lambda d, acc: acc + got[d], value)

    def gram_chunks(rows, local, which):
        value = dot(rows.T, rows)
        local[:, which] = value.reshape(n_k, chunk, rank)

    def gather_gram(full, value, stage):
        full[k] = value

        def one(d, carry):
            send(full.at[k], full.at[k], {"ka": rem(k + d, n_k)}, stage)
            return carry

        lax.fori_loop(1, n_k, one, 0)
        sends.append((full.at[pl.ds(0, n_k - 1)], stage))

    def invert_first(full):
        mat = full[...].reshape(rank, rank)
        pinv = inverse_half(mat[:HALF, :HALF])
        cross = mat[:HALF, HALF:]
        w = dot(pinv, cross)
        factor[0] = pinv
        factor[1] = w
        factor[2] = mat[HALF:, HALF:] - dot(cross.T, w)

    def invert_second():
        factor[2] = inverse_half(factor[2])

    def solve(rows):
        left, right = rows[:, :HALF], rows[:, HALF:]
        w = factor[1]
        v = dot(dot(left, w) - right, factor[2])
        return jnp.concatenate([dot(left, factor[0]) + dot_nt(v, w), -v], axis=1)

    def normalized(hat, got_k, mine_k, got_p, mine_p, stage):
        mine_k[...] = jnp.sum((hat * hat).reshape(piece // 8, 8, rank), axis=0)
        share_k(lambda to: mine_k, got_k, stage)
        mine_p[...] = total(mine_k[...], got_k, stage)
        share_plane(mine_p, got_p, stage + 1)
        squares = jnp.sum(total(mine_p[...], got_p, stage + 1), axis=0, keepdims=True)
        return hat / jnp.sqrt(squares / total_rows + EPS)

    def make_inner(s):
        x_copy(s).wait()
        c_rows = c_slab[third[s]].astype(jnp.bfloat16)
        span = 8

        def one(n, carry):
            rows = x_buf[s, pl.ds(n * span, span)].reshape(span * edge, edge)
            value = jnp.dot(rows, c_rows, preferred_element_type=F32)
            inner[s, pl.ds(n * span, span)] = value.reshape(span, edge, rank)
            return carry

        lax.fori_loop(0, edge // span, one, 0)

    def x_copy(s):
        return pltpu.make_async_copy(x_hbm.at[s], x_buf.at[s], copy_sem.at[s])

    def load_rows(buf, table, s):
        for t in range(per_block):
            value = buf[table[s * per_block + t]]
            rows_f32[s, pl.ds(t * piece, piece)] = value.astype(F32)

    def mode_one(s):
        def one(n, carry):
            span = 8
            for h in range(rank // HALF):
                lanes = pl.ds(h * HALF, HALF)
                value = inner[s, pl.ds(n * span, span), :, lanes]
                summed = jnp.sum(value * rows_f32[s, :, lanes][None], axis=1)
                contrib[s * per_block + div(n * span, piece), pl.ds(pl.multiple_of(rem(n * span, piece), span), span), lanes] = summed
            return carry

        lax.fori_loop(0, edge // 8, one, 0)

    def mode_two(s):
        def one(n, acc):
            for u in range(8):
                acc = acc + inner[s, n * 8 + u] * rows_f32[s, pl.ds(n * 8 + u, 1), :]
            return acc

        acc = lax.fori_loop(0, edge // 8, one, jnp.zeros((edge, rank), F32))
        contrib[pl.ds(s * per_block, per_block)] = acc.reshape(per_block, piece, rank)

    def place(table, part):
        def one(q, carry):
            part[q] = contrib[table[q]] + contrib[table[part.shape[0] + q]]
            return carry

        lax.fori_loop(0, part.shape[0], one, 0)

    for s in range(2):
        x_copy(s).start()
    gathered_b[(core * n_i + i) * n_z + z] = b_own[...].astype(jnp.bfloat16)
    barrier = pltpu.get_barrier_semaphore()

    def greet_k(d, carry):
        pl.semaphore_signal(barrier, inc=1, device_id={"ka": rem(k + d, n_k)}, device_id_type=MESH)
        return carry

    def greet_plane(d, carry):
        pl.semaphore_signal(barrier, inc=1, device_id=at_plane(rem(plane + d, n_plane)), device_id_type=MESH)
        return carry

    lax.fori_loop(1, n_k, greet_k, 0)
    lax.fori_loop(1, n_plane, greet_plane, 0)
    pl.semaphore_wait(barrier, n_k + n_plane - 2)

    gather_z(gathered_b, i, n_i, 0)
    gram_chunks(b_own[...], local1, 0)
    gram_chunks(c_slab[div(plane, per_block), pl.ds(pl.multiple_of(rem(plane, per_block) * piece, piece), piece)], local1, 1)
    share_k(lambda to: local1.at[to], gram1, 3)
    gather_line(gathered_b, "ia", i, n_i, 1)
    make_inner(0)
    gather_core(gathered_b, n_i, 2)
    make_inner(1)
    own1[...] = total(local1[k], gram1, 3)
    share_plane(own1, mix1, 4)
    contrib[2 * per_block] = jnp.zeros((piece, rank), F32)
    arrived(gathered_b.at[pl.ds(0, n_i * n_z)], 2)
    for s in range(2):
        load_rows(gathered_b, rows_b, s)
        mode_one(s)
    place(spots_one, part1)
    scatter_core(part1, core1, 6)
    grams = total(own1[...], mix1, 4)
    gram_c_own[...] = grams[1]
    gather_gram(full1, grams[0] * grams[1], 5)
    scatter_line(part1, core1, line1, "ja", j, n_j, 7)
    arrived(full1.at[pl.ds(0, n_k - 1)], 5)
    invert_first(full1)
    scatter_z(part1, line1, zed1, j, n_j, 8)
    invert_second()
    a_hat = solve(scatter_end(part1, zed1, j, n_j, 9))
    a_rows = normalized(a_hat, sq_ka.at[0], sq_kb.at[0], sq_la.at[0], sq_lb.at[0], 9)
    a_out[...] = a_rows

    gathered_a[(core * n_j + j) * n_z + z] = a_rows.astype(jnp.bfloat16)
    gather_z(gathered_a, j, n_j, 11)
    gram_chunks(a_rows, local2, 0)
    share_k(lambda to: local2.at[to], gram2, 14)
    gather_line(gathered_a, "ja", j, n_j, 12)
    own2[...] = total(local2[k], gram2, 14)
    share_plane(own2, mix2, 15)
    gather_core(gathered_a, n_j, 13)
    arrived(gathered_a.at[pl.ds(0, n_j * n_z)], 13)
    for s in range(2):
        load_rows(gathered_a, rows_a, s)
        mode_two(s)
    place(spots_two, part2)
    scatter_core(part2, core2, 17)
    gather_gram(full2, total(own2[...], mix2, 15)[0] * gram_c_own[...], 16)
    scatter_line(part2, core2, line2, "ia", i, n_i, 18)
    arrived(full2.at[pl.ds(0, n_k - 1)], 16)
    invert_first(full2)
    scatter_z(part2, line2, zed2, i, n_i, 19)
    invert_second()
    b_hat = solve(scatter_end(part2, zed2, i, n_i, 20))
    b_out[...] = normalized(b_hat, sq_ka.at[1], sq_kb.at[1], sq_la.at[1], sq_lb.at[1], 20)

    for like, stage in sends:
        pltpu.make_async_copy(like, like, send_sem.at[stage]).wait()


def tables(coord, filled, owner, per_block, n_k):
    count = owner.shape[0]
    place = jnp.arange(count, dtype=jnp.int32)
    wanted = (coord[:, None] * per_block + jnp.arange(per_block, dtype=jnp.int32)).reshape(-1)
    stored = jnp.sum(jnp.where(wanted[:, None] == place, owner, 0), axis=1)
    half = count // 2
    n_z = n_k // 2
    at = rem(stored, 2) * half + div(stored, n_k) * n_z + div(rem(stored, n_k), 2)
    live = (jnp.arange(2, dtype=jnp.int32) < filled)[:, None, None]
    hit = jnp.logical_and(at.reshape(2, per_block, 1) == place, live)
    none = 2 * per_block
    spots = none + jnp.sum(jnp.where(hit, jnp.arange(none, dtype=jnp.int32).reshape(2, per_block, 1) - none, 0), axis=1)
    return at, spots.reshape(-1)


def solution(mesh):
    n_i, n_j, n_k = (mesh.shape[name] for name in ("ia", "ja", "ka"))
    n_z = n_k // 2
    sizes = (n_i, n_j, n_k)

    def body(blocks, first, second, third, filled, owner_one, owner_two, factor_b, factor_c):
        piece, rank = factor_b.shape[1:]
        edge = blocks.shape[-1]
        chunk = rank // n_k
        n_plane = n_i * n_j
        stages = 22

        def vmem(*shape, dtype=F32):
            return pltpu.VMEM(shape, dtype)

        def scatter_buffers(n_line):
            return [
                vmem(2 * n_line * n_z, piece, rank),
                vmem(n_line * n_z, piece, rank),
                vmem(n_line - 1, n_z, piece, rank),
                vmem(n_z - 1, piece, rank),
            ]

        def gram_buffers(count):
            return [
                vmem(n_k, count, chunk, rank),
                vmem(n_k - 1, count, chunk, rank),
                vmem(n_plane - 1, count, chunk, rank),
                vmem(n_k, chunk, rank),
            ]

        scratch = [
            vmem(2, edge, edge, edge, dtype=jnp.bfloat16),
            vmem(2, edge, edge, rank),
            vmem(2 * n_i * n_z, piece, rank, dtype=jnp.bfloat16),
            vmem(2 * n_j * n_z, piece, rank, dtype=jnp.bfloat16),
            vmem(2, edge, rank),
            vmem(2 * edge // piece + 1, piece, rank),
            *scatter_buffers(n_j),
            *scatter_buffers(n_i),
            *gram_buffers(2),
            *gram_buffers(1),
            vmem(2, chunk, rank),
            vmem(1, chunk, rank),
            vmem(chunk, rank),
            vmem(2, n_k - 1, 8, rank),
            vmem(2, 8, rank),
            vmem(2, n_plane - 1, 8, rank),
            vmem(2, 8, rank),
            vmem(3, HALF, HALF),
            pltpu.SemaphoreType.DMA((2,)),
            pltpu.SemaphoreType.DMA((stages,)),
            pltpu.SemaphoreType.DMA((stages,)),
        ]
        per_block = edge // piece
        rows_b, spots_two = tables(second.reshape(2), filled.reshape(1), owner_two, per_block, n_k)
        rows_a, spots_one = tables(first.reshape(2), filled.reshape(1), owner_one, per_block, n_k)
        smem = pl.BlockSpec(memory_space=pltpu.SMEM)
        whole = pl.BlockSpec(memory_space=pltpu.VMEM)
        a_own, b_own = pl.pallas_call(
            functools.partial(kernel, sizes),
            out_shape=[jax.ShapeDtypeStruct((piece, rank), F32)] * 2,
            in_specs=[smem] * 5 + [pl.BlockSpec(memory_space=pl.ANY), whole, whole],
            out_specs=[whole, whole],
            scratch_shapes=scratch,
            compiler_params=pltpu.CompilerParams(
                collective_id=0, has_side_effects=True, vmem_limit_bytes=62 * 1024 * 1024
            ),
            name="sweep",
        )(
            third.reshape(2),
            rows_b,
            rows_a,
            spots_one,
            spots_two,
            blocks.reshape(blocks.shape[3:]),
            factor_b[0],
            factor_c[0].reshape(-1, edge, rank),
        )
        return a_own[None], b_own[None]

    return jax.shard_map(
        body,
        mesh=mesh,
        in_specs=(
            P("ia", "ja", "ka", None, None, None, None),
            P("ia", "ja", "ka", None),
            P("ia", "ja", "ka", None),
            P("ia", "ja", "ka", None),
            P("ia", "ja", "ka"),
            P(),
            P(),
            P("ja", ("ia", "ka"), None),
            P("ka", None, None),
        ),
        out_specs=(P("ia", ("ja", "ka"), None), P("ja", ("ia", "ka"), None)),
        check_vma=False,
    )
```

time: 837 us -> 155 us (0.19); the launches traced: 827 us -> 155 us
  waiting for transfers between devices: 447 us -> 0 us
  blocking collectives: 156 us -> 0 us
  Pallas kernels: 0 us -> 146 us
  other arithmetic: 133 us -> 3.81 us
  local copies, waits for them, and re-layouts: 42.5 us -> 4.31 us
  between operations: 19.3 us -> 1.3 us
  matrix products: 17.4 us -> 0 us
  loops' own time: 12.2 us -> 0 us
    psum x2 -> x0, waiting for transfers between devices: 300 us -> none  [the longest x1 150 us: body(): gram_a = lax.psum(local_a, ('ia', 'ja', 'ka'))]
    psum x2 -> x0, blocking collectives: 156 us -> none  [the longest x1 78 us: body(): squares_a = lax.psum(jnp.sum(a_hat * a_hat, axis=0), ('ia', 'ja', 'ka'))]
    all_gather x2 -> x0, waiting for transfers between devices: 147 us -> none  [the longest x1 75.5 us: body(): lax.all_gather(factor_b.astype(jnp.bfloat16), ('ia', 'ka'), axis=1, tiled...]
    pallas_call x0 -> x1, Pallas kernels: none -> 146 us  [body(): pl.pallas_call(functools.partial(kernel, sizes), out_shape=[jax.ShapeDtyp...]
    another operation x18 -> x0, other arithmetic: 108 us -> none  [the longest x13 68.6 us: solve_rows(): lower = jnp.linalg.cholesky(gram)]
    cond x4 -> x0, other arithmetic: 16.5 us -> none
    cond x8 -> x0, local copies, waits for them, and re-layouts: 13.6 us -> none
    another operation x6 -> x0, loops' own time: 12.2 us -> none  [the longest x2 10.9 us: solve_rows(): return jax.scipy.linalg.cho_solve((lower, True), rows.T).T]
  transfers between devices with their start and end apart: 6 -> 0, of which waited for: 4 -> 0; matrix products, arithmetic and copies ran while one was open for 22% -> 0% of each run, Pallas kernels for 0% -> 0%
where the time goes in v1:
time: 155 us
  Pallas kernels  146 us (94%)
  local copies, waits for them, and re-layouts  4.31 us (3%)
  other arithmetic  3.81 us (2%)
    pallas_call x1, Pallas kernels, body(): pl.pallas_call(functools.partial(kernel, sizes), out_shape=[jax.ShapeDtyp...  146 us

profile of v1, /device:TPU:1, one launch (start us, length us, event | category | flops | bytes accessed | tf_op | source)
XLA Modules:
  0.0 155.0 jit_solution(14418911790366383828)
XLA Ops:
  1.3 0.7 multiply_bitcast_fusion
  1.9 0.1 iota_add_fusion
  2.0 0.1 add.103
  2.1 0.8 select_reduce_fusion.2
  2.9 0.7 multiply_bitcast_fusion.1
  3.6 0.1 iota_add_fusion.1
  3.7 0.1 add.97
  3.8 0.8 select_reduce_fusion.3
  4.6 0.1 reduce_sum.44
  4.7 0.5 fusion.19
  5.2 0.1 reduce_sum.42
  5.3 0.1 select_reduce_fusion
  5.4 0.6 add.113.spots_two
  6.0 0.6 add.109.spots_one
  6.7 145.6 %sweep.1 = (f32[32,256]{1,0:T(8,128)}, f32[32,256]{1,0:T(8,128)}) custom-call(s32[2]{0:T(128)} %bitcast.17, s32[8]{0:T(128)} %get-tuple-element.10.rows_b, s32[8]{0:T(128)} %get-tuple-element.11.rows_a, s32[128]{0:T(128)} %add.109.spots_one, s32[128]{0:T(128)} %add.113.spots_two, bf16[2,128,128,128]{3,2,1,0:T(8,128)(2,1)} %bitcast.12, f32[32,256]{1,0:T(8,128)} %bitcast.14, ...), custom_call_target="tpu_custom_call" | custom-call | tf_op jit(solution)/shard_map/sweep/pallas_call | solution.py:467
  152.3 1.4 copy.14
  153.6 1.4 copy.15
  (5 shorter events, 0.1 us)

commit v2 on v1

--- a/solution.py
+++ b/solution.py
@@ -39,12 +39,15 @@
 
     def step(_, mat):
         top, rest = mat[:GROUP], mat[GROUP:]
+        spread = [jnp.broadcast_to(top[:, t : t + 1], (GROUP, HALF)) for t in range(GROUP)]
         for s in range(GROUP):
-            column = jnp.broadcast_to(top[:, s : s + 1], (GROUP, HALF))
+            column = spread[s]
             inv = 1.0 / column[s : s + 1]
             row = jnp.where(lane[:1] == s, 1.0, top[s : s + 1]) * inv
-            cleared = jnp.where(lane == s, 0.0, top)
-            top = jnp.where(sub == s, row, cleared - column * row)
+            top = jnp.where(sub == s, row, jnp.where(lane == s, 0.0, top) - column * row)
+            for t in range(s + 1, GROUP):
+                entry = spread[t][s : s + 1] * inv
+                spread[t] = jnp.where(sub == s, entry, spread[t] - column * entry)
         out = jnp.where(lane_rest < GROUP, 0.0, rest)
         for s in range(GROUP):
             out = out - rest[:, s : s + 1] * top[s : s + 1]
@@ -55,11 +58,12 @@
 
 def kernel(
     sizes,
+    filled,
+    first,
+    second,
     third,
-    rows_b,
-    rows_a,
-    spots_one,
-    spots_two,
+    owner_one,
+    owner_two,
     x_hbm,
     b_own,
     c_slab,
@@ -95,6 +99,8 @@
     sq_la,
     sq_lb,
     factor,
+    spots_one,
+    spots_two,
     copy_sem,
     send_sem,
     recv_sem,
@@ -113,6 +119,9 @@
     n_plane = n_i * n_j
     sends = []
 
+    def sent(pair):
+        sends.append(pair)
+
     def send(src, dst, where, stage):
         pltpu.make_async_remote_copy(
             src_ref=src,
@@ -137,30 +146,27 @@
             return carry
 
         lax.fori_loop(1, n_z, one, 0)
-        sends.append((buf.at[pl.ds(0, n_z - 1)], stage))
-
-    def gather_line(buf, axis, line, n_line, stage):
+        sent((buf.at[pl.ds(0, n_z - 1)], stage))
+
+    def gather_line(buf, axis, line, n_line, stage, lines):
         arrived(buf.at[pl.ds(0, n_z - 1)], stage - 1)
         mine = buf.at[pl.ds((core * n_line + line) * n_z, n_z)]
-
-        def one(d, carry):
-            send(mine, mine, {axis: rem(line + d, n_line)}, stage)
-            return carry
-
-        lax.fori_loop(1, n_line, one, 0)
-        sends.append((buf.at[pl.ds(0, (n_line - 1) * n_z)], stage))
-
-    def gather_core(buf, n_line, stage):
-        half = n_line * n_z
-        arrived(buf.at[pl.ds(0, half - n_z)], stage - 1)
-        mine = buf.at[pl.ds(core * half, half)]
+        for d in range(1, n_line):
+            send(mine, mine, {axis: rem(line + d, n_line)}, lines + d)
+            sent((buf.at[pl.ds(0, n_z)], lines + d))
         send(mine, mine, {"ka": z * 2 + 1 - core}, stage)
-        sends.append((buf.at[pl.ds(0, half)], stage))
+
+    def gather_core(buf, line, n_line, stage, lines):
+        for d in sorted(range(1, n_line), key=lambda d: min(d, n_line - d)):
+            arrived(buf.at[pl.ds(0, n_z)], lines + d)
+            mine = buf.at[pl.ds((core * n_line + rem(line + n_line - d, n_line)) * n_z, n_z)]
+            send(mine, mine, {"ka": z * 2 + 1 - core}, stage)
+        sent((buf.at[pl.ds(0, n_line * n_z)], stage))
 
     def scatter_core(part, got, stage):
         half = got.shape[0]
         send(part.at[pl.ds((1 - core) * half, half)], got, {"ka": z * 2 + 1 - core}, stage)
-        sends.append((got, stage))
+        sent((got, stage))
 
     def scatter_line(part, got_core, got, axis, line, n_line, stage):
         arrived(got_core, stage - 1)
@@ -178,7 +184,7 @@
             return carry
 
         lax.fori_loop(1, n_line, one, 0)
-        sends.append((got, stage))
+        sent((got, stage))
 
     def scatter_z(part, got_line, got, line, n_line, stage):
         arrived(got_line, stage - 1)
@@ -199,7 +205,7 @@
             return carry
 
         lax.fori_loop(1, n_z, one, 0)
-        sends.append((got, stage))
+        sent((got, stage))
 
     def scatter_end(part, got, line, n_line, stage):
         arrived(got, stage - 1)
@@ -214,7 +220,7 @@
             return carry
 
         lax.fori_loop(1, n_k, one, 0)
-        sends.append((got, stage))
+        sent((got, stage))
 
     def share_plane(source, got, stage):
         def one(d, carry):
@@ -222,7 +228,7 @@
             return carry
 
         lax.fori_loop(1, n_plane, one, 0)
-        sends.append((got, stage))
+        sent((got, stage))
 
     def total(value, got, stage):
         arrived(got, stage)
@@ -240,7 +246,7 @@
             return carry
 
         lax.fori_loop(1, n_k, one, 0)
-        sends.append((full.at[pl.ds(0, n_k - 1)], stage))
+        sent((full.at[pl.ds(0, n_k - 1)], stage))
 
     def invert_first(full):
         mat = full[...].reshape(rank, rank)
@@ -284,9 +290,12 @@
     def x_copy(s):
         return pltpu.make_async_copy(x_hbm.at[s], x_buf.at[s], copy_sem.at[s])
 
-    def load_rows(buf, table, s):
+    def position(stored, n_line):
+        return (rem(stored, 2) * n_line + div(stored, n_k)) * n_z + div(rem(stored, n_k), 2)
+
+    def load_rows(buf, coord, owner, n_line, s):
         for t in range(per_block):
-            value = buf[table[s * per_block + t]]
+            value = buf[position(owner[coord[s] * per_block + t], n_line)]
             rows_f32[s, pl.ds(t * piece, piece)] = value.astype(F32)
 
     def mode_one(s):
@@ -310,12 +319,31 @@
         acc = lax.fori_loop(0, edge // 8, one, jnp.zeros((edge, rank), F32))
         contrib[pl.ds(s * per_block, per_block)] = acc.reshape(per_block, piece, rank)
 
-    def place(table, part):
+    def find_spots(spots, coord, owner, n_line):
+        count = owner.shape[0]
+        none = 2 * per_block
+        wanted = [[position(owner[coord[s] * per_block + t], n_line) for t in range(per_block)] for s in range(2)]
+        live = [(s < filled[0]).astype(jnp.int32) for s in range(2)]
+
         def one(q, carry):
-            part[q] = contrib[table[q]] + contrib[table[part.shape[0] + q]]
-            return carry
-
-        lax.fori_loop(0, part.shape[0], one, 0)
+            for s in range(2):
+                at = jnp.int32(none)
+                for t in range(per_block):
+                    hit = (wanted[s][t] == q).astype(jnp.int32)
+                    at = at + hit * live[s] * (s * per_block + t - none)
+                spots[s * count + q] = at
+            return carry
+
+        lax.fori_loop(0, count, one, 0)
+
+    def place(spots, part):
+        count = part.shape[0]
+
+        def one(q, carry):
+            part[q] = contrib[spots[q]] + contrib[spots[count + q]]
+            return carry
+
+        lax.fori_loop(0, count, one, 0)
 
     for s in range(2):
         x_copy(s).start()
@@ -332,23 +360,26 @@
 
     lax.fori_loop(1, n_k, greet_k, 0)
     lax.fori_loop(1, n_plane, greet_plane, 0)
-    pl.semaphore_wait(barrier, n_k + n_plane - 2)
-
-    gather_z(gathered_b, i, n_i, 0)
     gram_chunks(b_own[...], local1, 0)
     gram_chunks(c_slab[div(plane, per_block), pl.ds(pl.multiple_of(rem(plane, per_block) * piece, piece), piece)], local1, 1)
+    pl.semaphore_wait(barrier, n_k + n_plane - 2)
+
+    gather_z(gathered_b, i, n_i, 0)
     share_k(lambda to: local1.at[to], gram1, 3)
-    gather_line(gathered_b, "ia", i, n_i, 1)
+    find_spots(spots_one, first, owner_one, n_j)
+    find_spots(spots_two, second, owner_two, n_i)
+    contrib[2 * per_block] = jnp.zeros((piece, rank), F32)
+    gather_line(gathered_b, "ia", i, n_i, 1, 22)
     make_inner(0)
-    gather_core(gathered_b, n_i, 2)
+    gather_core(gathered_b, i, n_i, 1, 22)
     make_inner(1)
+    arrived(gathered_b.at[pl.ds(0, n_i * n_z)], 1)
+    load_rows(gathered_b, second, owner_two, n_i, 0)
+    mode_one(0)
     own1[...] = total(local1[k], gram1, 3)
     share_plane(own1, mix1, 4)
-    contrib[2 * per_block] = jnp.zeros((piece, rank), F32)
-    arrived(gathered_b.at[pl.ds(0, n_i * n_z)], 2)
-    for s in range(2):
-        load_rows(gathered_b, rows_b, s)
-        mode_one(s)
+    load_rows(gathered_b, second, owner_two, n_i, 1)
+    mode_one(1)
     place(spots_one, part1)
     scatter_core(part1, core1, 6)
     grams = total(own1[...], mix1, 4)
@@ -367,13 +398,13 @@
     gather_z(gathered_a, j, n_j, 11)
     gram_chunks(a_rows, local2, 0)
     share_k(lambda to: local2.at[to], gram2, 14)
-    gather_line(gathered_a, "ja", j, n_j, 12)
+    gather_line(gathered_a, "ja", j, n_j, 12, 22 + n_i)
     own2[...] = total(local2[k], gram2, 14)
     share_plane(own2, mix2, 15)
-    gather_core(gathered_a, n_j, 13)
-    arrived(gathered_a.at[pl.ds(0, n_j * n_z)], 13)
+    gather_core(gathered_a, j, n_j, 12, 22 + n_i)
+    arrived(gathered_a.at[pl.ds(0, n_j * n_z)], 12)
     for s in range(2):
-        load_rows(gathered_a, rows_a, s)
+        load_rows(gathered_a, first, owner_one, n_j, s)
         mode_two(s)
     place(spots_two, part2)
     scatter_core(part2, core2, 17)
@@ -390,21 +421,6 @@
         pltpu.make_async_copy(like, like, send_sem.at[stage]).wait()
 
 
-def tables(coord, filled, owner, per_block, n_k):
-    count = owner.shape[0]
-    place = jnp.arange(count, dtype=jnp.int32)
-    wanted = (coord[:, None] * per_block + jnp.arange(per_block, dtype=jnp.int32)).reshape(-1)
-    stored = jnp.sum(jnp.where(wanted[:, None] == place, owner, 0), axis=1)
-    half = count // 2
-    n_z = n_k // 2
-    at = rem(stored, 2) * half + div(stored, n_k) * n_z + div(rem(stored, n_k), 2)
-    live = (jnp.arange(2, dtype=jnp.int32) < filled)[:, None, None]
-    hit = jnp.logical_and(at.reshape(2, per_block, 1) == place, live)
-    none = 2 * per_block
-    spots = none + jnp.sum(jnp.where(hit, jnp.arange(none, dtype=jnp.int32).reshape(2, per_block, 1) - none, 0), axis=1)
-    return at, spots.reshape(-1)
-
-
 def solution(mesh):
     n_i, n_j, n_k = (mesh.shape[name] for name in ("ia", "ja", "ka"))
     n_z = n_k // 2
@@ -415,7 +431,7 @@
         edge = blocks.shape[-1]
         chunk = rank // n_k
         n_plane = n_i * n_j
-        stages = 22
+        stages = 22 + n_i + n_j
 
         def vmem(*shape, dtype=F32):
             return pltpu.VMEM(shape, dtype)
@@ -455,19 +471,18 @@
             vmem(2, n_plane - 1, 8, rank),
             vmem(2, 8, rank),
             vmem(3, HALF, HALF),
+            pltpu.SMEM((2 * owner_one.shape[0],), jnp.int32),
+            pltpu.SMEM((2 * owner_two.shape[0],), jnp.int32),
             pltpu.SemaphoreType.DMA((2,)),
             pltpu.SemaphoreType.DMA((stages,)),
             pltpu.SemaphoreType.DMA((stages,)),
         ]
-        per_block = edge // piece
-        rows_b, spots_two = tables(second.reshape(2), filled.reshape(1), owner_two, per_block, n_k)
-        rows_a, spots_one = tables(first.reshape(2), filled.reshape(1), owner_one, per_block, n_k)
         smem = pl.BlockSpec(memory_space=pltpu.SMEM)
         whole = pl.BlockSpec(memory_space=pltpu.VMEM)
         a_own, b_own = pl.pallas_call(
             functools.partial(kernel, sizes),
             out_shape=[jax.ShapeDtypeStruct((piece, rank), F32)] * 2,
-            in_specs=[smem] * 5 + [pl.BlockSpec(memory_space=pl.ANY), whole, whole],
+            in_specs=[smem] * 6 + [pl.BlockSpec(memory_space=pl.ANY), whole, whole],
             out_specs=[whole, whole],
             scratch_shapes=scratch,
             compiler_params=pltpu.CompilerParams(
@@ -475,11 +490,12 @@
             ),
             name="sweep",
         )(
+            filled.reshape(1),
+            first.reshape(2),
+            second.reshape(2),
             third.reshape(2),
-            rows_b,
-            rows_a,
-            spots_one,
-            spots_two,
+            owner_one,
+            owner_two,
             blocks.reshape(blocks.shape[3:]),
             factor_b[0],
             factor_c[0].reshape(-1, edge, rank),

time: 155 us -> 132 us (0.85)
  Pallas kernels: 146 us -> 128 us
  other arithmetic: 3.81 us -> 0 us
  local copies, waits for them, and re-layouts: 4.31 us -> 2.75 us
    pallas_call x1, Pallas kernels: 146 us -> 128 us  [body(): pl.pallas_call(functools.partial(kernel, sizes), out_shape=[jax.ShapeDtyp...]
    reduce_sum x3 -> x0, other arithmetic: 1.76 us -> none  [the longest x2 1.67 us: tables(): stored = jnp.sum(jnp.where(wanted[:, None] == place, owner, 0), axis=1)]
where the time goes in v2:
time: 132 us
  Pallas kernels  128 us (97%)
  local copies, waits for them, and re-layouts  2.75 us (2%)
    pallas_call x1, Pallas kernels, body(): pl.pallas_call(functools.partial(kernel, sizes), out_shape=[jax.ShapeDtyp...  128 us
    unnamed x2, local copies, waits for them, and re-layouts  2.75 us

profile of v2, /device:TPU:1, one launch (start us, length us, event | category | flops | bytes accessed | tf_op | source)
XLA Modules:
  0.0 132.1 jit_solution(5527013235302463941)
XLA Ops:
  1.3 128.0 %sweep.1 = (f32[32,256]{1,0:T(8,128)}, f32[32,256]{1,0:T(8,128)}) custom-call(s32[1]{0:T(128)} %bitcast.9.filled, s32[2]{0:T(128)} %bitcast.15, s32[2]{0:T(128)} %bitcast.16, s32[2]{0:T(128)} %bitcast.17, s32[64]{0:T(128)} %owner_one.1, s32[64]{0:T(128)} %owner_two.1, bf16[2,128,128,128]{3,2,1,0:T(8,128)(2,1)} %bitcast.10, f32[32,256]{1,0:T(8,128)} %bitcast.12, ...), custom_call_target="tpu_custom_call" | custom-call | tf_op jit(solution)/shard_map/sweep/pallas_call | solution.py:482
  129.3 1.4 %copy.14 = f32[1,32,256]{2,1,0:T(8,128)} copy(f32[1,32,256]{2,1,0:T(8,128)} %bitcast.14) | data formatting | bytes 65536
  130.7 1.4 %copy.15 = f32[1,32,256]{2,1,0:T(8,128)} copy(f32[1,32,256]{2,1,0:T(8,128)} %bitcast.13) | data formatting | bytes 65536

commit v3 on v2

--- a/solution.py
+++ b/solution.py
@@ -98,6 +98,7 @@
     sq_kb,
     sq_la,
     sq_lb,
+    hats,
     factor,
     spots_one,
     spots_two,
@@ -149,7 +150,6 @@
         sent((buf.at[pl.ds(0, n_z - 1)], stage))
 
     def gather_line(buf, axis, line, n_line, stage, lines):
-        arrived(buf.at[pl.ds(0, n_z - 1)], stage - 1)
         mine = buf.at[pl.ds((core * n_line + line) * n_z, n_z)]
         for d in range(1, n_line):
             send(mine, mine, {axis: rem(line + d, n_line)}, lines + d)
@@ -266,13 +266,14 @@
         v = dot(dot(left, w) - right, factor[2])
         return jnp.concatenate([dot(left, factor[0]) + dot_nt(v, w), -v], axis=1)
 
-    def normalized(hat, got_k, mine_k, got_p, mine_p, stage):
-        mine_k[...] = jnp.sum((hat * hat).reshape(piece // 8, 8, rank), axis=0)
+    def squares_start(hat, got_k, mine_k, stage):
+        mine_k[...] = jnp.sum(hat * hat, axis=0, keepdims=True)
         share_k(lambda to: mine_k, got_k, stage)
+
+    def scale_of(got_k, mine_k, got_p, mine_p, stage):
         mine_p[...] = total(mine_k[...], got_k, stage)
         share_plane(mine_p, got_p, stage + 1)
-        squares = jnp.sum(total(mine_p[...], got_p, stage + 1), axis=0, keepdims=True)
-        return hat / jnp.sqrt(squares / total_rows + EPS)
+        return jnp.sqrt(total(mine_p[...], got_p, stage + 1) / total_rows + EPS)
 
     def make_inner(s):
         x_copy(s).wait()
@@ -369,6 +370,7 @@
     find_spots(spots_one, first, owner_one, n_j)
     find_spots(spots_two, second, owner_two, n_i)
     contrib[2 * per_block] = jnp.zeros((piece, rank), F32)
+    arrived(gathered_b.at[pl.ds(0, n_z - 1)], 0)
     gather_line(gathered_b, "ia", i, n_i, 1, 22)
     make_inner(0)
     gather_core(gathered_b, i, n_i, 1, 22)
@@ -391,14 +393,29 @@
     scatter_z(part1, line1, zed1, j, n_j, 8)
     invert_second()
     a_hat = solve(scatter_end(part1, zed1, j, n_j, 9))
-    a_rows = normalized(a_hat, sq_ka.at[0], sq_kb.at[0], sq_la.at[0], sq_lb.at[0], 9)
+    squares_start(a_hat, sq_ka.at[0], sq_kb.at[0], 9)
+    hats[z] = a_hat
+
+    def send_hat(d, carry):
+        send(hats.at[z], hats.at[z], {"ka": rem(z + d, n_z) * 2 + core}, 11)
+        return carry
+
+    lax.fori_loop(1, n_z, send_hat, 0)
+    sent((hats.at[pl.ds(0, n_z - 1)], 11))
+    scale_a = scale_of(sq_ka.at[0], sq_kb.at[0], sq_la.at[0], sq_lb.at[0], 9)
+    a_rows = a_hat / scale_a
     a_out[...] = a_rows
 
-    gathered_a[(core * n_j + j) * n_z + z] = a_rows.astype(jnp.bfloat16)
-    gather_z(gathered_a, j, n_j, 11)
+    arrived(hats.at[pl.ds(0, n_z - 1)], 11)
+
+    def to_half(p, carry):
+        gathered_a[(core * n_j + j) * n_z + p] = (hats[p] / scale_a).astype(jnp.bfloat16)
+        return carry
+
+    lax.fori_loop(0, n_z, to_half, 0)
+    gather_line(gathered_a, "ja", j, n_j, 12, 22 + n_i)
     gram_chunks(a_rows, local2, 0)
     share_k(lambda to: local2.at[to], gram2, 14)
-    gather_line(gathered_a, "ja", j, n_j, 12, 22 + n_i)
     own2[...] = total(local2[k], gram2, 14)
     share_plane(own2, mix2, 15)
     gather_core(gathered_a, j, n_j, 12, 22 + n_i)
@@ -415,7 +432,8 @@
     scatter_z(part2, line2, zed2, i, n_i, 19)
     invert_second()
     b_hat = solve(scatter_end(part2, zed2, i, n_i, 20))
-    b_out[...] = normalized(b_hat, sq_ka.at[1], sq_kb.at[1], sq_la.at[1], sq_lb.at[1], 20)
+    squares_start(b_hat, sq_ka.at[1], sq_kb.at[1], 20)
+    b_out[...] = b_hat / scale_of(sq_ka.at[1], sq_kb.at[1], sq_la.at[1], sq_lb.at[1], 20)
 
     for like, stage in sends:
         pltpu.make_async_copy(like, like, send_sem.at[stage]).wait()
@@ -466,10 +484,11 @@
             vmem(2, chunk, rank),
             vmem(1, chunk, rank),
             vmem(chunk, rank),
-            vmem(2, n_k - 1, 8, rank),
-            vmem(2, 8, rank),
-            vmem(2, n_plane - 1, 8, rank),
-            vmem(2, 8, rank),
+            vmem(2, n_k - 1, 1, rank),
+            vmem(2, 1, rank),
+            vmem(2, n_plane - 1, 1, rank),
+            vmem(2, 1, rank),
+            vmem(n_z, piece, rank),
             vmem(3, HALF, HALF),
             pltpu.SMEM((2 * owner_one.shape[0],), jnp.int32),
             pltpu.SMEM((2 * owner_two.shape[0],), jnp.int32),

time: 132 us -> 127 us (0.962)
  Pallas kernels: 128 us -> 123 us
    pallas_call x1, Pallas kernels: 128 us -> 123 us  [body(): pl.pallas_call(functools.partial(kernel, sizes), out_shape=[jax.ShapeDtyp...]
where the time goes in v3:
time: 127 us
  Pallas kernels  123 us (97%)
  local copies, waits for them, and re-layouts  2.75 us (2%)
  between operations  1.29 us (1%)
    pallas_call x1, Pallas kernels, body(): pl.pallas_call(functools.partial(kernel, sizes), out_shape=[jax.ShapeDtyp...  123 us
    unnamed x2, local copies, waits for them, and re-layouts  2.75 us

profile of v3, /device:TPU:1, one launch (start us, length us, event | category | flops | bytes accessed | tf_op | source)
XLA Modules:
  0.0 127.0 jit_solution(16533824992388970573)
XLA Ops:
  1.3 122.9 %sweep.1 = (f32[32,256]{1,0:T(8,128)}, f32[32,256]{1,0:T(8,128)}) custom-call(s32[1]{0:T(128)} %bitcast.9.filled, s32[2]{0:T(128)} %bitcast.15, s32[2]{0:T(128)} %bitcast.16, s32[2]{0:T(128)} %bitcast.17, s32[64]{0:T(128)} %owner_one.1, s32[64]{0:T(128)} %owner_two.1, bf16[2,128,128,128]{3,2,1,0:T(8,128)(2,1)} %bitcast.10, f32[32,256]{1,0:T(8,128)} %bitcast.12, ...), custom_call_target="tpu_custom_call" | custom-call | tf_op jit(solution)/shard_map/sweep/pallas_call | solution.py:501
  124.2 1.4 %copy.14 = f32[1,32,256]{2,1,0:T(8,128)} copy(f32[1,32,256]{2,1,0:T(8,128)} %bitcast.14) | data formatting | bytes 65536
  125.6 1.4 %copy.15 = f32[1,32,256]{2,1,0:T(8,128)} copy(f32[1,32,256]{2,1,0:T(8,128)} %bitcast.13) | data formatting | bytes 65536

commit v4 on v3

v4 whole, which is shorter than its diff:
```python
import functools

import jax
import jax.numpy as jnp
from jax import lax
from jax.experimental import pallas as pl
from jax.experimental.pallas import tpu as pltpu
from jax.sharding import PartitionSpec as P

EPS = 1e-06
HALF = 128
GROUP = 8
MESH = pl.DeviceIdType.MESH
F32 = jnp.float32


def rem(a, b):
    return lax.rem(a, jnp.int32(b))


def div(a, b):
    return lax.div(a, jnp.int32(b))


def dot(a, b):
    return jnp.dot(a, b, precision=lax.Precision.HIGHEST, preferred_element_type=F32)


def dot_nt(a, b):
    return lax.dot_general(
        a, b, (((1,), (1,)), ((), ())), precision=lax.Precision.HIGHEST, preferred_element_type=F32
    )


def inverse_half(mat):
    lane = lax.broadcasted_iota(jnp.int32, (GROUP, HALF), 1)
    sub = lax.broadcasted_iota(jnp.int32, (GROUP, HALF), 0)
    lane_rest = lax.broadcasted_iota(jnp.int32, (HALF - GROUP, HALF), 1)

    def step(_, mat):
        top, rest = mat[:GROUP], mat[GROUP:]
        spread = [jnp.broadcast_to(top[:, t : t + 1], (GROUP, HALF)) for t in range(GROUP)]
        for s in range(GROUP):
            column = spread[s]
            inv = 1.0 / column[s : s + 1]
            row = jnp.where(lane[:1] == s, 1.0, top[s : s + 1]) * inv
            top = jnp.where(sub == s, row, jnp.where(lane == s, 0.0, top) - column * row)
            for t in range(s + 1, GROUP):
                entry = spread[t][s : s + 1] * inv
                spread[t] = jnp.where(sub == s, entry, spread[t] - column * entry)
        out = jnp.where(lane_rest < GROUP, 0.0, rest)
        for s in range(GROUP):
            out = out - rest[:, s : s + 1] * top[s : s + 1]
        return pltpu.roll(jnp.concatenate([out, top], axis=0), HALF - GROUP, 1)

    return lax.fori_loop(0, HALF // GROUP, step, mat)


def kernel(
    sizes,
    filled,
    first,
    second,
    third,
    owner_one,
    owner_two,
    x_hbm,
    b_own,
    c_slab,
    a_out,
    b_out,
    x_buf,
    x_far,
    c_own,
    c_send,
    c_far,
    info_send,
    info_got,
    info,
    b_send,
    hat_send,
    inner,
    gathered_b,
    gathered_a,
    rows_f32,
    contrib,
    part1,
    line1,
    zed1,
    part2,
    line2,
    zed2,
    local1,
    gram1,
    mix1,
    full1,
    local2,
    gram2,
    mix2,
    full2,
    own1,
    own2,
    gram_c_own,
    sq_ka,
    sq_kb,
    sq_la,
    sq_lb,
    hats,
    factor,
    spots_one,
    spots_two,
    copy_sem,
    send_sem,
    recv_sem,
):
    n_i, n_j, n_k = sizes
    piece, rank = b_own.shape
    edge = x_hbm.shape[-1]
    per_block = edge // piece
    total_rows = n_i * n_j * n_k * piece
    chunk = rank // n_k
    i, j, k = lax.axis_index("ia"), lax.axis_index("ja"), lax.axis_index("ka")
    core = rem(k, 2)
    plane = i * n_j + j
    n_plane = n_i * n_j
    sends = []

    def sent(pair):
        sends.append(pair)

    def send(src, dst, where, stage):
        pltpu.make_async_remote_copy(
            src_ref=src,
            dst_ref=dst,
            send_sem=send_sem.at[stage],
            recv_sem=recv_sem.at[stage],
            device_id=where,
            device_id_type=MESH,
        ).start()

    def arrived(like, stage):
        pltpu.make_async_copy(like, like, recv_sem.at[stage]).wait()

    def at_plane(g):
        return {"ia": div(g, n_j), "ja": rem(g, n_j)}

    def send_halves(source, target, stage):
        def one(d, carry):
            to = rem(k + d, n_k)
            send(source.at[rem(to, 2)], target, {"ka": to}, stage)
            return carry

        lax.fori_loop(1, n_k, one, 0)

    def gather_line(buf, axis, line, n_line, stage):
        mine = buf.at[pl.ds(line * n_k, n_k)]

        def one(d, carry):
            send(mine, mine, {axis: rem(line + d, n_line)}, stage)
            return carry

        lax.fori_loop(1, n_line, one, 0)
        sent((buf.at[pl.ds(0, (n_line - 1) * n_k)], stage))

    def scatter_line(part, got, axis, line, n_line, stage):
        def one(d, carry):
            to = rem(line + d, n_line)
            send(part.at[pl.ds(to * n_k, n_k)], got.at[d - 1], {axis: to}, stage)
            return carry

        lax.fori_loop(1, n_line, one, 0)
        sent((got, stage))

    def scatter_k(part, got_line, got, line, n_line, stage):
        arrived(got_line, stage - 1)
        base = line * n_k

        def add(p, carry):
            value = part[base + p]
            for d in range(n_line - 1):
                value = value + got_line[d, p]
            part[base + p] = value
            return carry

        lax.fori_loop(0, n_k, add, 0)

        def one(d, carry):
            to = rem(k + d, n_k)
            send(part.at[base + to], got.at[d - 1], {"ka": to}, stage)
            return carry

        lax.fori_loop(1, n_k, one, 0)
        sent((got, stage))

    def scatter_end(part, got, line, stage):
        arrived(got, stage)
        same = part[line * n_k + k]
        other = got[0]
        for d in range(2, n_k):
            if d % 2 == 0:
                same = same + got[d - 1]
            else:
                other = other + got[d - 1]
        return jnp.concatenate([jnp.where(core == 0, same, other), jnp.where(core == 0, other, same)], axis=1)

    def mine_of(value):
        return jnp.where(core == 0, value[:, :HALF], value[:, HALF:])

    def halves(buf, value):
        buf[0] = value[:, :HALF]
        buf[1] = value[:, HALF:]

    def share_k(source, got, stage):
        def one(d, carry):
            send(source(rem(k + d, n_k)), got.at[d - 1], {"ka": rem(k + d, n_k)}, stage)
            return carry

        lax.fori_loop(1, n_k, one, 0)
        sent((got, stage))

    def share_plane(source, got, stage):
        def one(d, carry):
            send(source, got.at[d - 1], at_plane(rem(plane + d, n_plane)), stage)
            return carry

        lax.fori_loop(1, n_plane, one, 0)
        sent((got, stage))

    def total(value, got, stage):
        arrived(got, stage)
        return lax.fori_loop(0, got.shape[0], lambda d, acc: acc + got[d], value)

    def gram_chunks(rows, local, which):
        value = dot(rows.T, rows)
        local[:, which] = value.reshape(n_k, chunk, rank)

    def gather_gram(full, value, stage):
        full[k] = value

        def one(d, carry):
            send(full.at[k], full.at[k], {"ka": rem(k + d, n_k)}, stage)
            return carry

        lax.fori_loop(1, n_k, one, 0)
        sent((full.at[pl.ds(0, n_k - 1)], stage))

    def invert_first(full):
        mat = full[...].reshape(rank, rank)
        pinv = inverse_half(mat[:HALF, :HALF])
        cross = mat[:HALF, HALF:]
        w = dot(pinv, cross)
        factor[0] = pinv
        factor[1] = w
        factor[2] = mat[HALF:, HALF:] - dot(cross.T, w)

    def invert_second():
        factor[2] = inverse_half(factor[2])

    def solve(rows):
        left, right = rows[:, :HALF], rows[:, HALF:]
        w = factor[1]
        v = dot(dot(left, w) - right, factor[2])
        return jnp.concatenate([dot(left, factor[0]) + dot_nt(v, w), -v], axis=1)

    def squares_start(hat, got_k, mine_k, stage):
        mine_k[...] = jnp.sum(hat * hat, axis=0, keepdims=True)
        share_k(lambda to: mine_k, got_k, stage)

    def scale_of(got_k, mine_k, got_p, mine_p, stage):
        mine_p[...] = total(mine_k[...], got_k, stage)
        share_plane(mine_p, got_p, stage + 1)
        return jnp.sqrt(total(mine_p[...], got_p, stage + 1) / total_rows + EPS)

    def make_inner(s):
        c_rows = c_own[s] if s < 2 else c_far[s - 2]
        x_rows = x_buf if s < 2 else x_far
        span = 8

        def one(n, carry):
            rows = x_rows[s % 2, pl.ds(n * span, span)].reshape(span * edge, edge)
            value = jnp.dot(rows, c_rows, preferred_element_type=F32)
            inner[s, pl.ds(n * span, span)] = value.reshape(span, edge, HALF)
            return carry

        lax.fori_loop(0, edge // span, one, 0)

    def x_copy(s):
        return pltpu.make_async_copy(x_hbm.at[s], x_buf.at[s], copy_sem.at[s])

    def coord_of(near, at, s):
        return near[s] if s < 2 else info[0, at + s - 2]

    def load_rows(buf, near, at, owner, s):
        coord = coord_of(near, at, s)
        for t in range(per_block):
            rows_f32[s, pl.ds(t * piece, piece)] = buf[owner[coord * per_block + t]].astype(F32)

    def mode_one(s):
        def one(n, carry):
            span = 8
            summed = jnp.sum(inner[s, pl.ds(n * span, span)] * rows_f32[s][None], axis=1)
            at = s * per_block + div(n * span, piece)
            contrib[at, pl.ds(pl.multiple_of(rem(n * span, piece), span), span)] = summed
            return carry

        lax.fori_loop(0, edge // 8, one, 0)

    def mode_two(s):
        def one(n, acc):
            for u in range(8):
                acc = acc + inner[s, n * 8 + u] * rows_f32[s, pl.ds(n * 8 + u, 1), :]
            return acc

        acc = lax.fori_loop(0, edge // 8, one, jnp.zeros((edge, HALF), F32))
        contrib[pl.ds(s * per_block, per_block)] = acc.reshape(per_block, piece, HALF)

    def find_spots(spots, near, at, owner):
        count = owner.shape[0]
        none = 4 * per_block
        wanted = [[owner[coord_of(near, at, s) * per_block + t] for t in range(per_block)] for s in range(4)]
        live = [(s < filled[0]).astype(jnp.int32) if s < 2 else info[0, s - 2] for s in range(4)]

        def one(q, carry):
            for s in range(4):
                spot = jnp.int32(none)
                for t in range(per_block):
                    hit = (wanted[s][t] == q).astype(jnp.int32)
                    spot = spot + hit * live[s] * (s * per_block + t - none)
                spots[s * count + q] = spot
            return carry

        lax.fori_loop(0, count, one, 0)

    def place(spots, part):
        count = part.shape[0]

        def one(q, carry):
            value = contrib[spots[q]]
            for s in range(1, 4):
                value = value + contrib[spots[s * count + q]]
            part[q] = value
            return carry

        lax.fori_loop(0, count, one, 0)

    for s in range(2):
        x_copy(s).start()
    b_half = b_own[...].astype(jnp.bfloat16)
    halves(b_send, b_half)
    gathered_b[i * n_k + k] = mine_of(b_half)
    lane = lax.broadcasted_iota(jnp.int32, info_send.shape, 1)
    told = jnp.zeros(info_send.shape, jnp.int32)
    for s in range(2):
        told = jnp.where(lane == s, (s < filled[0]).astype(jnp.int32), told)
        told = jnp.where(lane == 2 + s, first[s], told)
        told = jnp.where(lane == 4 + s, second[s], told)
        rows = c_slab[third[s]].astype(jnp.bfloat16)
        c_own[s] = mine_of(rows)
        c_send[s] = jnp.where(core == 0, rows[:, HALF:], rows[:, :HALF])
    info_send[...] = told
    barrier = pltpu.get_barrier_semaphore()

    def greet_k(d, carry):
        pl.semaphore_signal(barrier, inc=1, device_id={"ka": rem(k + d, n_k)}, device_id_type=MESH)
        return carry

    def greet_plane(d, carry):
        pl.semaphore_signal(barrier, inc=1, device_id=at_plane(rem(plane + d, n_plane)), device_id_type=MESH)
        return carry

    lax.fori_loop(1, n_k, greet_k, 0)
    lax.fori_loop(1, n_plane, greet_plane, 0)
    gram_chunks(b_own[...], local1, 0)
    gram_chunks(c_slab[div(plane, per_block), pl.ds(pl.multiple_of(rem(plane, per_block) * piece, piece), piece)], local1, 1)
    pl.semaphore_wait(barrier, n_k + n_plane - 2)

    partner = {"ka": k + 1 - 2 * core}
    send_halves(b_send, gathered_b.at[i * n_k + k], 0)
    sent((gathered_b.at[pl.ds(0, n_k - 1)], 0))
    send(info_send, info_got, partner, 12)
    sent((info_got, 12))
    send(c_send, c_far, partner, 6)
    sent((c_far, 6))
    for s in range(2):
        send(x_hbm.at[s], x_far.at[s], partner, 1 + s)
        sent((x_far.at[s], 1 + s))
    share_k(lambda to: local1.at[to], gram1, 3)
    contrib[4 * per_block] = jnp.zeros((piece, HALF), F32)
    arrived(gathered_b.at[pl.ds(0, n_k - 1)], 0)
    gather_line(gathered_b, "ia", i, n_i, 13)
    x_copy(0).wait()
    make_inner(0)
    x_copy(1).wait()
    make_inner(1)
    arrived(info_got, 12)
    copy = pltpu.make_async_copy(info_got, info, copy_sem.at[2])
    copy.start()
    copy.wait()
    find_spots(spots_one, first, 2, owner_one)
    find_spots(spots_two, second, 4, owner_two)
    arrived(gathered_b.at[pl.ds(0, (n_i - 1) * n_k)], 13)
    for s in range(2):
        load_rows(gathered_b, second, 4, owner_two, s)
        mode_one(s)
    arrived(c_far, 6)
    for s in range(2, 4):
        arrived(x_far.at[s - 2], s - 1)
        make_inner(s)
        load_rows(gathered_b, second, 4, owner_two, s)
        mode_one(s)
        if s == 2:
            own1[...] = total(local1[k], gram1, 3)
            share_plane(own1, mix1, 4)
    place(spots_one, part1)
    scatter_line(part1, line1, "ja", j, n_j, 7)
    grams = total(own1[...], mix1, 4)
    gram_c_own[...] = grams[1]
    gather_gram(full1, grams[0] * grams[1], 5)
    arrived(full1.at[pl.ds(0, n_k - 1)], 5)
    invert_first(full1)
    scatter_k(part1, line1, zed1, j, n_j, 8)
    invert_second()
    a_hat = solve(scatter_end(part1, zed1, j, 8))
    squares_start(a_hat, sq_ka.at[0], sq_kb.at[0], 9)
    halves(hat_send, a_hat)
    hats[k] = mine_of(a_hat)
    send_halves(hat_send, hats.at[k], 11)
    sent((hats.at[pl.ds(0, n_k - 1)], 11))
    scale_a = scale_of(sq_ka.at[0], sq_kb.at[0], sq_la.at[0], sq_lb.at[0], 9)
    scale_own = mine_of(scale_a)
    arrived(hats.at[pl.ds(0, n_k - 1)], 11)

    def to_half(p, carry):
        gathered_a[j * n_k + p] = (hats[p] / scale_own).astype(jnp.bfloat16)
        return carry

    lax.fori_loop(0, n_k, to_half, 0)
    gather_line(gathered_a, "ja", j, n_j, 17)
    a_rows = a_hat / scale_a
    a_out[...] = a_rows
    gram_chunks(a_rows, local2, 0)
    share_k(lambda to: local2.at[to], gram2, 14)
    arrived(gathered_a.at[pl.ds(0, (n_j - 1) * n_k)], 17)
    for s in range(4):
        load_rows(gathered_a, first, 2, owner_one, s)
        mode_two(s)
        if s == 2:
            own2[...] = total(local2[k], gram2, 14)
            share_plane(own2, mix2, 15)
    place(spots_two, part2)
    scatter_line(part2, line2, "ia", i, n_i, 18)
    gather_gram(full2, total(own2[...], mix2, 15)[0] * gram_c_own[...], 16)
    arrived(full2.at[pl.ds(0, n_k - 1)], 16)
    invert_first(full2)
    scatter_k(part2, line2, zed2, i, n_i, 19)
    invert_second()
    b_hat = solve(scatter_end(part2, zed2, i, 19))
    squares_start(b_hat, sq_ka.at[1], sq_kb.at[1], 20)
    b_out[...] = b_hat / scale_of(sq_ka.at[1], sq_kb.at[1], sq_la.at[1], sq_lb.at[1], 20)

    for like, stage in sends:
        pltpu.make_async_copy(like, like, send_sem.at[stage]).wait()


def solution(mesh):
    n_i, n_j, n_k = (mesh.shape[name] for name in ("ia", "ja", "ka"))
    sizes = (n_i, n_j, n_k)

    def body(blocks, first, second, third, filled, owner_one, owner_two, factor_b, factor_c):
        piece, rank = factor_b.shape[1:]
        edge = blocks.shape[-1]
        chunk = rank // n_k
        n_plane = n_i * n_j
        stages = 22

        def vmem(*shape, dtype=F32):
            return pltpu.VMEM(shape, dtype)

        def scatter_buffers(n_line):
            return [
                vmem(n_line * n_k, piece, HALF),
                vmem(n_line - 1, n_k, piece, HALF),
                vmem(n_k - 1, piece, HALF),
            ]

        def gram_buffers(count):
            return [
                vmem(n_k, count, chunk, rank),
                vmem(n_k - 1, count, chunk, rank),
                vmem(n_plane - 1, count, chunk, rank),
                vmem(n_k, chunk, rank),
            ]

        scratch = [
            vmem(2, edge, edge, edge, dtype=jnp.bfloat16),
            vmem(2, edge, edge, edge, dtype=jnp.bfloat16),
            vmem(2, edge, HALF, dtype=jnp.bfloat16),
            vmem(2, edge, HALF, dtype=jnp.bfloat16),
            vmem(2, edge, HALF, dtype=jnp.bfloat16),
            vmem(8, HALF, dtype=jnp.int32),
            vmem(8, HALF, dtype=jnp.int32),
            pltpu.SMEM((8, HALF), jnp.int32),
            vmem(2, piece, HALF, dtype=jnp.bfloat16),
            vmem(2, piece, HALF),
            vmem(4, edge, edge, HALF),
            vmem(n_i * n_k, piece, HALF, dtype=jnp.bfloat16),
            vmem(n_j * n_k, piece, HALF, dtype=jnp.bfloat16),
            vmem(4, edge, HALF),
            vmem(4 * edge // piece + 1, piece, HALF),
            *scatter_buffers(n_j),
            *scatter_buffers(n_i),
            *gram_buffers(2),
            *gram_buffers(1),
            vmem(2, chunk, rank),
            vmem(1, chunk, rank),
            vmem(chunk, rank),
            vmem(2, n_k - 1, 1, rank),
            vmem(2, 1, rank),
            vmem(2, n_plane - 1, 1, rank),
            vmem(2, 1, rank),
            vmem(n_k, piece, HALF),
            vmem(3, HALF, HALF),
            pltpu.SMEM((4 * owner_one.shape[0],), jnp.int32),
            pltpu.SMEM((4 * owner_two.shape[0],), jnp.int32),
            pltpu.SemaphoreType.DMA((3,)),
            pltpu.SemaphoreType.DMA((stages,)),
            pltpu.SemaphoreType.DMA((stages,)),
        ]
        smem = pl.BlockSpec(memory_space=pltpu.SMEM)
        whole = pl.BlockSpec(memory_space=pltpu.VMEM)
        a_own, b_own = pl.pallas_call(
            functools.partial(kernel, sizes),
            out_shape=[jax.ShapeDtypeStruct((piece, rank), F32)] * 2,
            in_specs=[smem] * 6 + [pl.BlockSpec(memory_space=pl.ANY), whole, whole],
            out_specs=[whole, whole],
            scratch_shapes=scratch,
            compiler_params=pltpu.CompilerParams(
                collective_id=0, has_side_effects=True, vmem_limit_bytes=62 * 1024 * 1024
            ),
            name="sweep",
        )(
            filled.reshape(1),
            first.reshape(2),
            second.reshape(2),
            third.reshape(2),
            owner_one,
            owner_two,
            blocks.reshape(blocks.shape[3:]),
            factor_b[0],
            factor_c[0].reshape(-1, edge, rank),
        )
        return a_own[None], b_own[None]

    return jax.shard_map(
        body,
        mesh=mesh,
        in_specs=(
            P("ia", "ja", "ka", None, None, None, None),
            P("ia", "ja", "ka", None),
            P("ia", "ja", "ka", None),
            P("ia", "ja", "ka", None),
            P("ia", "ja", "ka"),
            P(),
            P(),
            P("ja", ("ia", "ka"), None),
            P("ka", None, None),
        ),
        out_specs=(P("ia", ("ja", "ka"), None), P("ja", ("ia", "ka"), None)),
        check_vma=False,
    )
```

time: 127 us -> 139 us (1.094)
  Pallas kernels: 123 us -> 135 us
    pallas_call x1, Pallas kernels: 123 us -> 135 us  [body(): pl.pallas_call(functools.partial(kernel, sizes), out_shape=[jax.ShapeDtyp...]
where the time goes in v4:
time: 139 us
  Pallas kernels  135 us (97%)
  local copies, waits for them, and re-layouts  2.75 us (2%)
    pallas_call x1, Pallas kernels, body(): pl.pallas_call(functools.partial(kernel, sizes), out_shape=[jax.ShapeDtyp...  135 us

profile of v4, /device:TPU:1, one launch (start us, length us, event | category | flops | bytes accessed | tf_op | source)
XLA Modules:
  0.0 138.6 jit_solution(10225464585318734695)
XLA Ops:
  1.3 134.5 %sweep.1 = (f32[32,256]{1,0:T(8,128)}, f32[32,256]{1,0:T(8,128)}) custom-call(s32[1]{0:T(128)} %bitcast.9.filled, s32[2]{0:T(128)} %bitcast.15, s32[2]{0:T(128)} %bitcast.16, s32[2]{0:T(128)} %bitcast.17, s32[64]{0:T(128)} %owner_one.1, s32[64]{0:T(128)} %owner_two.1, bf16[2,128,128,128]{3,2,1,0:T(8,128)(2,1)} %bitcast.10, f32[32,256]{1,0:T(8,128)} %bitcast.12, ...), custom_call_target="tpu_custom_call" | custom-call | tf_op jit(solution)/shard_map/sweep/pallas_call | solution.py:531
  135.8 1.4 copy.14
  137.2 1.4 copy.15

commit v5 on v3

--- a/solution.py
+++ b/solution.py
@@ -119,6 +119,8 @@
     plane = i * n_j + j
     n_plane = n_i * n_j
     sends = []
+    extra = 22 + n_i + n_j
+    extra2 = extra + n_j + n_z // 2
 
     def sent(pair):
         sends.append(pair)
@@ -163,53 +165,52 @@
             send(mine, mine, {"ka": z * 2 + 1 - core}, stage)
         sent((buf.at[pl.ds(0, n_line * n_z)], stage))
 
-    def scatter_core(part, got, stage):
-        half = got.shape[0]
-        send(part.at[pl.ds((1 - core) * half, half)], got, {"ka": z * 2 + 1 - core}, stage)
+    pair = 2
+
+    def scatter_core(part, got, spots, line, n_line, stage):
+        for d in [*range(1, n_line), 0]:
+            at = rem(line + d, n_line) * n_z
+            far = (1 - core) * n_line * n_z + at
+            place(spots, part, far)
+            send(part.at[pl.ds(far, n_z)], got.at[pl.ds(at, n_z)], {"ka": z * 2 + 1 - core}, stage + d)
+            sent((got.at[pl.ds(0, n_z)], stage + d))
+        for d in range(n_line):
+            place(spots, part, (core * n_line + rem(line + d, n_line)) * n_z)
+
+    def add_core(part, got_core, line, n_line, d, stage):
+        at = rem(line + d, n_line) * n_z
+        arrived(got_core.at[pl.ds(0, n_z)], stage + d)
+        mine = pl.ds(core * n_line * n_z + at, n_z)
+        part[mine] = part[mine] + got_core[pl.ds(at, n_z)]
+
+    def scatter_line(part, got_core, got, axis, line, n_line, core_stage, stage):
+        for d in range(1, n_line):
+            add_core(part, got_core, line, n_line, d, core_stage)
+            to = rem(line + d, n_line)
+            base = (core * n_line + to) * n_z
+            for g in range(n_z // pair):
+                send(part.at[pl.ds(base + g * pair, pair)], got.at[g, d - 1], {axis: to}, stage + g)
+        for g in range(n_z // pair):
+            sent((got.at[g], stage + g))
+        add_core(part, got_core, line, n_line, 0, core_stage)
+
+    def scatter_z(part, got_line, got, line, n_line, line_stage, stage):
+        base = (core * n_line + line) * n_z
+        for g in range(n_z // pair):
+            arrived(got_line.at[g], line_stage + g)
+            group = pl.ds(base + g * pair, pair)
+            value = part[group]
+            for d in range(n_line - 1):
+                value = value + got_line[g, d]
+            part[group] = value
+            for p in range(g * pair, (g + 1) * pair):
+                if p < n_z - 1:
+                    send(part.at[base + p], got.at[p], {"ka": rem(z + p + 1, n_z) * 2 + core}, stage)
         sent((got, stage))
 
-    def scatter_line(part, got_core, got, axis, line, n_line, stage):
-        arrived(got_core, stage - 1)
-        half = n_line * n_z
-
-        def add(p, carry):
-            part[core * half + p] = part[core * half + p] + got_core[p]
-            return carry
-
-        lax.fori_loop(0, half, add, 0)
-
-        def one(d, carry):
-            to = rem(line + d, n_line)
-            send(part.at[pl.ds(core * half + to * n_z, n_z)], got.at[d - 1], {axis: to}, stage)
-            return carry
-
-        lax.fori_loop(1, n_line, one, 0)
-        sent((got, stage))
-
-    def scatter_z(part, got_line, got, line, n_line, stage):
-        arrived(got_line, stage - 1)
-        base = (core * n_line + line) * n_z
-
-        def add(p, carry):
-            value = part[base + p]
-            for d in range(n_line - 1):
-                value = value + got_line[d, p]
-            part[base + p] = value
-            return carry
-
-        lax.fori_loop(0, n_z, add, 0)
-
-        def one(d, carry):
-            to = rem(z + d, n_z)
-            send(part.at[base + to], got.at[d - 1], {"ka": to * 2 + core}, stage)
-            return carry
-
-        lax.fori_loop(1, n_z, one, 0)
-        sent((got, stage))
-
     def scatter_end(part, got, line, n_line, stage):
-        arrived(got, stage - 1)
-        value = part[(core * n_line + line) * n_z + z]
+        arrived(got, stage)
+        value = part[(core * n_line + line) * n_z + n_z - 1]
         for d in range(n_z - 1):
             value = value + got[d]
         return value
@@ -337,14 +338,15 @@
 
         lax.fori_loop(0, count, one, 0)
 
-    def place(spots, part):
+    def place(spots, part, start):
         count = part.shape[0]
 
-        def one(q, carry):
-            part[q] = contrib[spots[q]] + contrib[spots[count + q]]
-            return carry
-
-        lax.fori_loop(0, count, one, 0)
+        def one(p, carry):
+            q = start + rem(z + 1 + p, n_z)
+            part[start + p] = contrib[spots[q]] + contrib[spots[count + q]]
+            return carry
+
+        lax.fori_loop(0, n_z, one, 0)
 
     for s in range(2):
         x_copy(s).start()
@@ -382,17 +384,16 @@
     share_plane(own1, mix1, 4)
     load_rows(gathered_b, second, owner_two, n_i, 1)
     mode_one(1)
-    place(spots_one, part1)
-    scatter_core(part1, core1, 6)
+    scatter_core(part1, core1, spots_one, j, n_j, extra)
     grams = total(own1[...], mix1, 4)
     gram_c_own[...] = grams[1]
     gather_gram(full1, grams[0] * grams[1], 5)
-    scatter_line(part1, core1, line1, "ja", j, n_j, 7)
+    scatter_line(part1, core1, line1, "ja", j, n_j, extra, extra + n_j)
     arrived(full1.at[pl.ds(0, n_k - 1)], 5)
     invert_first(full1)
-    scatter_z(part1, line1, zed1, j, n_j, 8)
+    scatter_z(part1, line1, zed1, j, n_j, extra + n_j, 8)
     invert_second()
-    a_hat = solve(scatter_end(part1, zed1, j, n_j, 9))
+    a_hat = solve(scatter_end(part1, zed1, j, n_j, 8))
     squares_start(a_hat, sq_ka.at[0], sq_kb.at[0], 9)
     hats[z] = a_hat
 
@@ -416,22 +417,21 @@
     gather_line(gathered_a, "ja", j, n_j, 12, 22 + n_i)
     gram_chunks(a_rows, local2, 0)
     share_k(lambda to: local2.at[to], gram2, 14)
+    gather_core(gathered_a, j, n_j, 12, 22 + n_i)
     own2[...] = total(local2[k], gram2, 14)
     share_plane(own2, mix2, 15)
-    gather_core(gathered_a, j, n_j, 12, 22 + n_i)
     arrived(gathered_a.at[pl.ds(0, n_j * n_z)], 12)
     for s in range(2):
         load_rows(gathered_a, first, owner_one, n_j, s)
         mode_two(s)
-    place(spots_two, part2)
-    scatter_core(part2, core2, 17)
+    scatter_core(part2, core2, spots_two, i, n_i, extra2)
     gather_gram(full2, total(own2[...], mix2, 15)[0] * gram_c_own[...], 16)
-    scatter_line(part2, core2, line2, "ia", i, n_i, 18)
+    scatter_line(part2, core2, line2, "ia", i, n_i, extra2, extra2 + n_i)
     arrived(full2.at[pl.ds(0, n_k - 1)], 16)
     invert_first(full2)
-    scatter_z(part2, line2, zed2, i, n_i, 19)
+    scatter_z(part2, line2, zed2, i, n_i, extra2 + n_i, 19)
     invert_second()
-    b_hat = solve(scatter_end(part2, zed2, i, n_i, 20))
+    b_hat = solve(scatter_end(part2, zed2, i, n_i, 19))
     squares_start(b_hat, sq_ka.at[1], sq_kb.at[1], 20)
     b_out[...] = b_hat / scale_of(sq_ka.at[1], sq_kb.at[1], sq_la.at[1], sq_lb.at[1], 20)
 
@@ -449,7 +449,7 @@
         edge = blocks.shape[-1]
         chunk = rank // n_k
         n_plane = n_i * n_j
-        stages = 22 + n_i + n_j
+        stages = 22 + 2 * (n_i + n_j) + n_z // 2 * 2
 
         def vmem(*shape, dtype=F32):
             return pltpu.VMEM(shape, dtype)
@@ -458,7 +458,7 @@
             return [
                 vmem(2 * n_line * n_z, piece, rank),
                 vmem(n_line * n_z, piece, rank),
-                vmem(n_line - 1, n_z, piece, rank),
+                vmem(n_z // 2, n_line - 1, 2, piece, rank),
                 vmem(n_z - 1, piece, rank),
             ]
 

time: 127 us -> 126 us (level)
    pallas_call x1, Pallas kernels: 123 us -> 122 us  [body(): pl.pallas_call(functools.partial(kernel, sizes), out_shape=[jax.ShapeDtyp...]
where the time goes in v5:
time: 126 us
  Pallas kernels  122 us (97%)
  local copies, waits for them, and re-layouts  2.75 us (2%)
  between operations  1.29 us (1%)
    pallas_call x1, Pallas kernels, body(): pl.pallas_call(functools.partial(kernel, sizes), out_shape=[jax.ShapeDtyp...  122 us
    unnamed x2, local copies, waits for them, and re-layouts  2.75 us

profile of v5, /device:TPU:1, one launch (start us, length us, event | category | flops | bytes accessed | tf_op | source)
XLA Modules:
  0.0 125.6 jit_solution(4383273271083402920)
XLA Ops:
  1.3 121.6 %sweep.1 = (f32[32,256]{1,0:T(8,128)}, f32[32,256]{1,0:T(8,128)}) custom-call(s32[1]{0:T(128)} %bitcast.9.filled, s32[2]{0:T(128)} %bitcast.15, s32[2]{0:T(128)} %bitcast.16, s32[2]{0:T(128)} %bitcast.17, s32[64]{0:T(128)} %owner_one.1, s32[64]{0:T(128)} %owner_two.1, bf16[2,128,128,128]{3,2,1,0:T(8,128)(2,1)} %bitcast.10, f32[32,256]{1,0:T(8,128)} %bitcast.12, ...), custom_call_target="tpu_custom_call" | custom-call | tf_op jit(solution)/shard_map/sweep/pallas_call | solution.py:501
  122.9 1.4 %copy.14 = f32[1,32,256]{2,1,0:T(8,128)} copy(f32[1,32,256]{2,1,0:T(8,128)} %bitcast.14) | data formatting | bytes 65536
  124.2 1.4 %copy.15 = f32[1,32,256]{2,1,0:T(8,128)} copy(f32[1,32,256]{2,1,0:T(8,128)} %bitcast.13) | data formatting | bytes 65536

commit v6 on v5

--- a/solution.py
+++ b/solution.py
@@ -22,6 +22,11 @@
     return lax.div(a, jnp.int32(b))
 
 
+def each(count, one):
+    for d in range(1, count):
+        one(d, 0)
+
+
 def dot(a, b):
     return jnp.dot(a, b, precision=lax.Precision.HIGHEST, preferred_element_type=F32)
 
@@ -32,7 +37,7 @@
     )
 
 
-def inverse_half(mat):
+def inverse_half(mat, start=0, stop=HALF // GROUP):
     lane = lax.broadcasted_iota(jnp.int32, (GROUP, HALF), 1)
     sub = lax.broadcasted_iota(jnp.int32, (GROUP, HALF), 0)
     lane_rest = lax.broadcasted_iota(jnp.int32, (HALF - GROUP, HALF), 1)
@@ -53,7 +58,7 @@
             out = out - rest[:, s : s + 1] * top[s : s + 1]
         return pltpu.roll(jnp.concatenate([out, top], axis=0), HALF - GROUP, 1)
 
-    return lax.fori_loop(0, HALF // GROUP, step, mat)
+    return lax.fori_loop(start, stop, step, mat)
 
 
 def kernel(
@@ -148,7 +153,7 @@
             send(mine, mine, {"ka": rem(z + d, n_z) * 2 + core}, stage)
             return carry
 
-        lax.fori_loop(1, n_z, one, 0)
+        each(n_z, one)
         sent((buf.at[pl.ds(0, n_z - 1)], stage))
 
     def gather_line(buf, axis, line, n_line, stage, lines):
@@ -194,9 +199,9 @@
             sent((got.at[g], stage + g))
         add_core(part, got_core, line, n_line, 0, core_stage)
 
-    def scatter_z(part, got_line, got, line, n_line, line_stage, stage):
+    def scatter_z(part, got_line, got, line, n_line, line_stage, stage, groups):
         base = (core * n_line + line) * n_z
-        for g in range(n_z // pair):
+        for g in groups:
             arrived(got_line.at[g], line_stage + g)
             group = pl.ds(base + g * pair, pair)
             value = part[group]
@@ -206,7 +211,8 @@
             for p in range(g * pair, (g + 1) * pair):
                 if p < n_z - 1:
                     send(part.at[base + p], got.at[p], {"ka": rem(z + p + 1, n_z) * 2 + core}, stage)
-        sent((got, stage))
+        if n_z // pair - 1 in groups:
+            sent((got, stage))
 
     def scatter_end(part, got, line, n_line, stage):
         arrived(got, stage)
@@ -220,7 +226,7 @@
             send(source(rem(k + d, n_k)), got.at[d - 1], {"ka": rem(k + d, n_k)}, stage)
             return carry
 
-        lax.fori_loop(1, n_k, one, 0)
+        each(n_k, one)
         sent((got, stage))
 
     def share_plane(source, got, stage):
@@ -228,7 +234,7 @@
             send(source, got.at[d - 1], at_plane(rem(plane + d, n_plane)), stage)
             return carry
 
-        lax.fori_loop(1, n_plane, one, 0)
+        each(n_plane, one)
         sent((got, stage))
 
     def total(value, got, stage):
@@ -246,17 +252,20 @@
             send(full.at[k], full.at[k], {"ka": rem(k + d, n_k)}, stage)
             return carry
 
-        lax.fori_loop(1, n_k, one, 0)
+        each(n_k, one)
         sent((full.at[pl.ds(0, n_k - 1)], stage))
 
-    def invert_first(full):
+    def invert_first(full, between):
         mat = full[...].reshape(rank, rank)
-        pinv = inverse_half(mat[:HALF, :HALF])
-        cross = mat[:HALF, HALF:]
+        middle = HALF // GROUP // 2
+        factor[0] = inverse_half(mat[:HALF, :HALF], 0, middle)
+        between()
+        pinv = inverse_half(factor[0], middle)
+        cross = full[...].reshape(rank, rank)[:HALF, HALF:]
         w = dot(pinv, cross)
         factor[0] = pinv
         factor[1] = w
-        factor[2] = mat[HALF:, HALF:] - dot(cross.T, w)
+        factor[2] = full[...].reshape(rank, rank)[HALF:, HALF:] - dot(cross.T, w)
 
     def invert_second():
         factor[2] = inverse_half(factor[2])
@@ -364,7 +373,7 @@
     lax.fori_loop(1, n_k, greet_k, 0)
     lax.fori_loop(1, n_plane, greet_plane, 0)
     gram_chunks(b_own[...], local1, 0)
-    gram_chunks(c_slab[div(plane, per_block), pl.ds(pl.multiple_of(rem(plane, per_block) * piece, piece), piece)], local1, 1)
+    gram_chunks(c_slab[...].reshape(-1, rank), local1, 1)
     pl.semaphore_wait(barrier, n_k + n_plane - 2)
 
     gather_z(gathered_b, i, n_i, 0)
@@ -380,18 +389,21 @@
     arrived(gathered_b.at[pl.ds(0, n_i * n_z)], 1)
     load_rows(gathered_b, second, owner_two, n_i, 0)
     mode_one(0)
-    own1[...] = total(local1[k], gram1, 3)
+    grams = total(local1[k], gram1, 3)
+    own1[...] = grams[:1]
+    gram_c_own[...] = grams[1]
     share_plane(own1, mix1, 4)
     load_rows(gathered_b, second, owner_two, n_i, 1)
     mode_one(1)
     scatter_core(part1, core1, spots_one, j, n_j, extra)
-    grams = total(own1[...], mix1, 4)
-    gram_c_own[...] = grams[1]
-    gather_gram(full1, grams[0] * grams[1], 5)
+    gather_gram(full1, total(own1[...], mix1, 4)[0] * gram_c_own[...], 5)
     scatter_line(part1, core1, line1, "ja", j, n_j, extra, extra + n_j)
+    groups = list(range(n_z // pair))
+    on_one = functools.partial(scatter_z, part1, line1, zed1, j, n_j, extra + n_j, 8)
+    on_one(groups[:-2])
     arrived(full1.at[pl.ds(0, n_k - 1)], 5)
-    invert_first(full1)
-    scatter_z(part1, line1, zed1, j, n_j, extra + n_j, 8)
+    invert_first(full1, lambda: on_one(groups[-2:-1]))
+    on_one(groups[-1:])
     invert_second()
     a_hat = solve(scatter_end(part1, zed1, j, n_j, 8))
     squares_start(a_hat, sq_ka.at[0], sq_kb.at[0], 9)
@@ -401,7 +413,7 @@
         send(hats.at[z], hats.at[z], {"ka": rem(z + d, n_z) * 2 + core}, 11)
         return carry
 
-    lax.fori_loop(1, n_z, send_hat, 0)
+    each(n_z, send_hat)
     sent((hats.at[pl.ds(0, n_z - 1)], 11))
     scale_a = scale_of(sq_ka.at[0], sq_kb.at[0], sq_la.at[0], sq_lb.at[0], 9)
     a_rows = a_hat / scale_a
@@ -427,9 +439,11 @@
     scatter_core(part2, core2, spots_two, i, n_i, extra2)
     gather_gram(full2, total(own2[...], mix2, 15)[0] * gram_c_own[...], 16)
     scatter_line(part2, core2, line2, "ia", i, n_i, extra2, extra2 + n_i)
+    on_two = functools.partial(scatter_z, part2, line2, zed2, i, n_i, extra2 + n_i, 19)
+    on_two(groups[:-2])
     arrived(full2.at[pl.ds(0, n_k - 1)], 16)
-    invert_first(full2)
-    scatter_z(part2, line2, zed2, i, n_i, extra2 + n_i, 19)
+    invert_first(full2, lambda: on_two(groups[-2:-1]))
+    on_two(groups[-1:])
     invert_second()
     b_hat = solve(scatter_end(part2, zed2, i, n_i, 19))
     squares_start(b_hat, sq_ka.at[1], sq_kb.at[1], 20)
@@ -466,7 +480,7 @@
             return [
                 vmem(n_k, count, chunk, rank),
                 vmem(n_k - 1, count, chunk, rank),
-                vmem(n_plane - 1, count, chunk, rank),
+                vmem(n_plane - 1, 1, chunk, rank),
                 vmem(n_k, chunk, rank),
             ]
 
@@ -481,7 +495,7 @@
             *scatter_buffers(n_i),
             *gram_buffers(2),
             *gram_buffers(1),
-            vmem(2, chunk, rank),
+            vmem(1, chunk, rank),
             vmem(1, chunk, rank),
             vmem(chunk, rank),
             vmem(2, n_k - 1, 1, rank),

time: 126 us -> 123 us (0.976)
  Pallas kernels: 122 us -> 119 us
    pallas_call x1, Pallas kernels: 122 us -> 119 us  [body(): pl.pallas_call(functools.partial(kernel, sizes), out_shape=[jax.ShapeDtyp...]
where the time goes in v6:
time: 123 us
  Pallas kernels  119 us (97%)
  local copies, waits for them, and re-layouts  2.75 us (2%)
  between operations  1.29 us (1%)
    pallas_call x1, Pallas kernels, body(): pl.pallas_call(functools.partial(kernel, sizes), out_shape=[jax.ShapeDtyp...  119 us
    unnamed x2, local copies, waits for them, and re-layouts  2.75 us

profile of v6, /device:TPU:1, one launch (start us, length us, event | category | flops | bytes accessed | tf_op | source)
XLA Modules:
  0.0 122.6 jit_solution(10536424175013546181)
XLA Ops:
  1.3 118.6 %sweep.1 = (f32[32,256]{1,0:T(8,128)}, f32[32,256]{1,0:T(8,128)}) custom-call(s32[1]{0:T(128)} %bitcast.9.filled, s32[2]{0:T(128)} %bitcast.15, s32[2]{0:T(128)} %bitcast.16, s32[2]{0:T(128)} %bitcast.17, s32[64]{0:T(128)} %owner_one.1, s32[64]{0:T(128)} %owner_two.1, bf16[2,128,128,128]{3,2,1,0:T(8,128)(2,1)} %bitcast.10, f32[32,256]{1,0:T(8,128)} %bitcast.12, ...), custom_call_target="tpu_custom_call" | custom-call | tf_op jit(solution)/shard_map/sweep/pallas_call | solution.py:515
  119.9 1.4 %copy.14 = f32[1,32,256]{2,1,0:T(8,128)} copy(f32[1,32,256]{2,1,0:T(8,128)} %bitcast.14) | data formatting | bytes 65536
  121.3 1.4 %copy.15 = f32[1,32,256]{2,1,0:T(8,128)} copy(f32[1,32,256]{2,1,0:T(8,128)} %bitcast.13) | data formatting | bytes 65536
